TPU v7x, 32 devices: a whole 2x2x4 slice. The times are simulated.
32 devices in a mesh: dp: 8 (over y, x, core), inner: 4 (over z).
Axes of the slice: x: 2, y: 2, z: 4, core: 2. Of those that a mesh axis runs over, the one named last changes fastest.
Arguments:
- tokens: bfloat16 [32, 1024, 768], P(('dp', 'inner')), may hold values from -6 to 6
- lengths: int32 [32], P(('dp', 'inner')), may hold values from 512 to 1024, as said below
- cotangent: bfloat16 [32, 1024, 768], P(('dp', 'inner')), may hold values from -6 to 6
- norm1_gain: bfloat16 [768], P(('dp', 'inner')), may hold values from 0.5 to 1.5
- norm1_bias: bfloat16 [768], P(('dp', 'inner')), may hold values from -1.5 to 1.5
- attn_in: bfloat16 [768, 2304], P(('dp', 'inner')), may hold values from -0.21875 to 0.21875
- attn_bias: bfloat16 [1536], P(('dp', 'inner')), may hold values from -2.5 to 2.5
- attn_out: bfloat16 [768, 768], P(('dp', 'inner')), may hold values from -1.75 to 1.75
- out_bias: bfloat16 [768], P(('dp', 'inner')), may hold values from -1.5 to 1.5
- norm2_gain: bfloat16 [768], P(('dp', 'inner')), may hold values from 0.5 to 1.5
- norm2_bias: bfloat16 [768], P(('dp', 'inner')), may hold values from -1.5 to 1.5
- mlp_up: bfloat16 [768, 3072], P(('dp', 'inner')), may hold values from -0.21875 to 0.21875
- up_bias: bfloat16 [3072], P(('dp', 'inner')), may hold values from -2.5 to 2.5
- mlp_down: bfloat16 [3072, 768], P(('dp', 'inner')), may hold values from -0.21875 to 0.21875
- down_bias: bfloat16 [768], P(('dp', 'inner')), may hold values from -1.5 to 1.5
Outputs:
- output: bfloat16 [32, 1024, 768], P(('dp', 'inner'))
- tokens_grad: bfloat16 [32, 1024, 768], P(('dp', 'inner'))
- norm1_gain_grad: float32 [768], P(('dp', 'inner'))
- norm1_bias_grad: float32 [768], P(('dp', 'inner'))
- attn_in_grad: float32 [768, 2304], P(('dp', 'inner'))
- attn_bias_grad: float32 [1536], P(('dp', 'inner'))
- attn_out_grad: float32 [768, 768], P(('dp', 'inner'))
- out_bias_grad: float32 [768], P(('dp', 'inner'))
- norm2_gain_grad: float32 [768], P(('dp', 'inner'))
- norm2_bias_grad: float32 [768], P(('dp', 'inner'))
- mlp_up_grad: float32 [768, 3072], P(('dp', 'inner'))
- up_bias_grad: float32 [3072], P(('dp', 'inner'))
- mlp_down_grad: float32 [3072, 768], P(('dp', 'inner'))
- down_bias_grad: float32 [768], P(('dp', 'inner'))
Inputs may be any that keep to these rules, and one draw needn't show every extreme that they name: `lengths`: each length is 1024 or 512, and exactly half of the sequences have each.
All inputs are finite; a program needn't handle non-finite values.
Results may differ from a plain program's by a relative error of at most 0.011.
Values may be sent and summed in bfloat16 or wider, within the bound.
No kernel may reach another device: no remote copies, remote signals or barrier semaphores. Data moves between devices by JAX's collectives and lax.ppermute only.
A program may use at most 256 MiB of HBM per device.

v0:
```python
import jax
import jax.numpy as jnp
from jax import lax
from jax.sharding import PartitionSpec as P

EPSILON = 1e-05
SCALE = 0.125
MASKED = -1000000000.0


def norm_rows(values, gain, shift):
    centre = values - jnp.mean(values, axis=-1, keepdims=True)
    spread = jnp.mean(centre * centre, axis=-1, keepdims=True)
    return centre * lax.rsqrt(spread + EPSILON) * gain + shift


def gelu_tanh(values):
    return (
        0.5
        * values
        * (1.0 + jnp.tanh(0.7978845608028654 * (values + 0.044715 * values * values * values)))
    )


def matmul(left, right):
    return jnp.dot(left, right, preferred_element_type=jnp.float32)


def matmul_tr(left, right):
    return lax.dot_general(
        left, right, (((1,), (1,)), ((), ())), preferred_element_type=jnp.float32
    )


def tr_matmul(left, right):
    return lax.dot_general(
        left, right, (((0,), (0,)), ((), ())), preferred_element_type=jnp.float32
    )


def fetch_attention(gain_one, shift_one, w_in, bias_in, w_out, bias_out):
    return (
        lax.all_gather(gain_one, ("dp", "inner"), axis=0, tiled=True),
        lax.all_gather(shift_one, ("dp", "inner"), axis=0, tiled=True),
        lax.all_gather(w_in, ("dp", "inner"), axis=0, tiled=True),
        lax.all_gather(bias_in, ("dp", "inner"), axis=0, tiled=True),
        lax.all_gather(w_out, ("dp", "inner"), axis=0, tiled=True),
        lax.all_gather(bias_out, ("dp", "inner"), axis=0, tiled=True),
    )


def fetch_forward(gain_two, shift_two, w_up, bias_up, w_down, bias_down):
    return (
        lax.all_gather(gain_two, ("dp", "inner"), axis=0, tiled=True),
        lax.all_gather(shift_two, ("dp", "inner"), axis=0, tiled=True),
        lax.all_gather(w_up, ("dp", "inner"), axis=0, tiled=True),
        lax.all_gather(bias_up, ("dp", "inner"), axis=0, tiled=True),
        lax.all_gather(w_down, ("dp", "inner"), axis=0, tiled=True),
        lax.all_gather(bias_down, ("dp", "inner"), axis=0, tiled=True),
    )


def reduce_forward(gain_grad, shift_grad, up_grad, up_bias_grad, down_grad, down_bias_grad):
    return (
        lax.psum_scatter(gain_grad, ("dp", "inner"), scatter_dimension=0, tiled=True),
        lax.psum_scatter(shift_grad, ("dp", "inner"), scatter_dimension=0, tiled=True),
        lax.psum_scatter(up_grad, ("dp", "inner"), scatter_dimension=0, tiled=True),
        lax.psum_scatter(up_bias_grad, ("dp", "inner"), scatter_dimension=0, tiled=True),
        lax.psum_scatter(down_grad, ("dp", "inner"), scatter_dimension=0, tiled=True),
        lax.psum_scatter(down_bias_grad, ("dp", "inner"), scatter_dimension=0, tiled=True),
    )


def reduce_attention(gain_grad, shift_grad, in_grad, bias_in_grad, out_grad, out_bias_grad):
    return (
        lax.psum_scatter(gain_grad, ("dp", "inner"), scatter_dimension=0, tiled=True),
        lax.psum_scatter(shift_grad, ("dp", "inner"), scatter_dimension=0, tiled=True),
        lax.psum_scatter(in_grad, ("dp", "inner"), scatter_dimension=0, tiled=True),
        lax.psum_scatter(bias_in_grad, ("dp", "inner"), scatter_dimension=0, tiled=True),
        lax.psum_scatter(out_grad, ("dp", "inner"), scatter_dimension=0, tiled=True),
        lax.psum_scatter(out_bias_grad, ("dp", "inner"), scatter_dimension=0, tiled=True),
    )


def masked_scores(queries, key_rows, start):
    scores = (
        jnp.einsum("qhd,khd->hqk", queries, key_rows, preferred_element_type=jnp.float32) * SCALE
    )
    row_places = start + jnp.arange(queries.shape[0], dtype=jnp.int32)
    col_places = jnp.arange(key_rows.shape[0], dtype=jnp.int32)
    allowed = col_places[None, :] <= row_places[:, None]
    return (jnp.where(allowed[None], scores, MASKED), row_places)


def attend(queries, key_rows, value_rows, start, count):
    scores, row_places = masked_scores(queries, key_rows, start)
    top_score = jnp.max(scores, axis=-1, keepdims=True)
    expo = jnp.exp(scores - top_score)
    row_total = jnp.sum(expo, axis=-1, keepdims=True)
    probs = expo / row_total
    log_total = (top_score + jnp.log(row_total))[..., 0]
    mixed = jnp.einsum(
        "hqk,khd->qhd", probs.astype(jnp.bfloat16), value_rows, preferred_element_type=jnp.float32
    )
    live_rows = (row_places < count).astype(jnp.float32)
    return (mixed * live_rows[:, None, None], log_total)


def attend_back(queries, key_rows, value_rows, grad_mixed, log_total, start):
    scores, row_places = masked_scores(queries, key_rows, start)
    probs = jnp.exp(scores - log_total[..., None])
    value_grad = jnp.einsum(
        "hqk,qhd->khd", probs.astype(jnp.bfloat16), grad_mixed, preferred_element_type=jnp.float32
    )
    prob_grad = jnp.einsum(
        "qhd,khd->hqk", grad_mixed, value_rows, preferred_element_type=jnp.float32
    )
    inner_sum = jnp.sum(probs * prob_grad, axis=-1, keepdims=True)
    score_grad = (probs * (prob_grad - inner_sum)).astype(jnp.bfloat16)
    query_grad = (
        jnp.einsum("hqk,khd->qhd", score_grad, key_rows, preferred_element_type=jnp.float32) * SCALE
    )
    key_grad = (
        jnp.einsum("hqk,qhd->khd", score_grad, queries, preferred_element_type=jnp.float32) * SCALE
    )
    return (query_grad, key_grad, value_grad)


def local(
    tokens,
    lengths,
    cotangent,
    norm1_gain,
    norm1_bias,
    attn_in,
    attn_bias,
    attn_out,
    out_bias,
    norm2_gain,
    norm2_bias,
    mlp_up,
    up_bias,
    mlp_down,
    down_bias,
):
    attn_set = fetch_attention(norm1_gain, norm1_bias, attn_in, attn_bias, attn_out, out_bias)
    mlp_set = fetch_forward(norm2_gain, norm2_bias, mlp_up, up_bias, mlp_down, down_bias)
    gain_one, shift_one, w_in, bias_in, w_out, bias_out = attn_set
    gain_two, shift_two, w_up, bias_up, w_down, bias_down = mlp_set
    inputs = tokens[0].astype(jnp.float32)
    count = lengths[0]
    rows = inputs.shape[0]
    width = inputs.shape[1]
    heads = width // 64
    block_rows = min(512, rows)
    num_blocks = rows // block_rows
    gain_first = gain_one.astype(jnp.float32)
    shift_first = shift_one.astype(jnp.float32)
    normed1 = norm_rows(inputs, gain_first, shift_first).astype(jnp.bfloat16)
    zero_bias = jnp.zeros((width,), jnp.float32)
    bias_float = bias_in.astype(jnp.float32)
    full_bias = jnp.concatenate([bias_float[:width], zero_bias, bias_float[width:]])
    qkv = (matmul(normed1, w_in) + full_bias).astype(jnp.bfloat16)
    queries = qkv[:, :width].reshape(rows, heads, 64)
    key_rows = qkv[:, width : 2 * width].reshape(rows, heads, 64)
    value_rows = qkv[:, 2 * width :].reshape(rows, heads, 64)
    mixed_blocks = []
    log_blocks = []
    for number in range(num_blocks):
        start = number * block_rows
        key_end = start + block_rows
        query_block = queries[start:key_end]
        key_block = key_rows[:key_end]
        value_block = value_rows[:key_end]

        def compute_block():
            return attend(query_block, key_block, value_block, start, count)

        def empty_block():
            return (
                jnp.zeros((block_rows, heads, 64), jnp.float32),
                jnp.zeros((heads, block_rows), jnp.float32),
            )

        if number == 0:
            mixed_part, log_part = compute_block()
        else:
            mixed_part, log_part = lax.cond(start < count, compute_block, empty_block)
        mixed_blocks.append(mixed_part)
        log_blocks.append(log_part)
    mixed = jnp.concatenate(mixed_blocks, axis=0).reshape(rows, width).astype(jnp.bfloat16)
    resid = inputs + matmul(mixed, w_out) + bias_out.astype(jnp.float32)
    gain_second = gain_two.astype(jnp.float32)
    shift_second = shift_two.astype(jnp.float32)
    normed2 = norm_rows(resid, gain_second, shift_second).astype(jnp.bfloat16)
    hidden = matmul(normed2, w_up) + bias_up.astype(jnp.float32)
    activated = gelu_tanh(hidden).astype(jnp.bfloat16)
    output = (resid + matmul(activated, w_down) + bias_down.astype(jnp.float32)).astype(
        jnp.bfloat16
    )
    back_attn = (
        lax.all_gather(norm1_gain, ("dp", "inner"), axis=0, tiled=True),
        lax.all_gather(norm1_bias, ("dp", "inner"), axis=0, tiled=True),
        lax.all_gather(attn_in, ("dp", "inner"), axis=0, tiled=True),
        lax.all_gather(attn_bias, ("dp", "inner"), axis=0, tiled=True),
        lax.all_gather(attn_out, ("dp", "inner"), axis=0, tiled=True),
        lax.all_gather(out_bias, ("dp", "inner"), axis=0, tiled=True),
    )
    back_mlp = (
        lax.all_gather(norm2_gain, ("dp", "inner"), axis=0, tiled=True),
        lax.all_gather(norm2_bias, ("dp", "inner"), axis=0, tiled=True),
        lax.all_gather(mlp_up, ("dp", "inner"), axis=0, tiled=True),
        lax.all_gather(up_bias, ("dp", "inner"), axis=0, tiled=True),
        lax.all_gather(mlp_down, ("dp", "inner"), axis=0, tiled=True),
        lax.all_gather(down_bias, ("dp", "inner"), axis=0, tiled=True),
    )
    w_in_back = back_attn[2]
    w_out_back = back_attn[4]
    w_up_back = back_mlp[2]
    w_down_back = back_mlp[4]
    grad_out = cotangent[0]
    grad_float = grad_out.astype(jnp.float32)
    down_grad = tr_matmul(activated, grad_out)
    down_bias_grad = jnp.sum(grad_float, axis=0)
    act_grad = matmul_tr(grad_out, w_down_back)
    gelu_value, gelu_pull = jax.vjp(gelu_tanh, hidden)
    hidden_grad = gelu_pull(act_grad)[0].astype(jnp.bfloat16)
    up_grad = tr_matmul(normed2, hidden_grad)
    up_bias_grad = jnp.sum(hidden_grad.astype(jnp.float32), axis=0)
    normed2_grad = matmul_tr(hidden_grad, w_up_back)
    norm_value, norm_pull = jax.vjp(norm_rows, resid, gain_second, shift_second)
    resid_part, gain_two_grad, shift_two_grad = norm_pull(normed2_grad)
    resid_grad = grad_float + resid_part
    resid_low = resid_grad.astype(jnp.bfloat16)
    out_grad = tr_matmul(mixed, resid_low)
    out_bias_grad = jnp.sum(resid_low.astype(jnp.float32), axis=0)
    places = jnp.arange(rows, dtype=jnp.int32)
    live_rows = (places < count).astype(jnp.bfloat16)
    mixed_grad = (
        matmul_tr(resid_low, w_out_back).astype(jnp.bfloat16) * live_rows[:, None]
    ).reshape(rows, heads, 64)
    key_total = jnp.zeros((rows, heads, 64), jnp.float32)
    value_total = jnp.zeros((rows, heads, 64), jnp.float32)
    query_blocks = []
    for number in range(num_blocks):
        start = number * block_rows
        key_end = start + block_rows
        query_block = queries[start:key_end]
        key_block = key_rows[:key_end]
        value_block = value_rows[:key_end]
        grad_block = mixed_grad[start:key_end]
        log_block = log_blocks[number]

        def compute_back():
            return attend_back(query_block, key_block, value_block, grad_block, log_block, start)

        def empty_back():
            return (
                jnp.zeros((block_rows, heads, 64), jnp.float32),
                jnp.zeros((key_end, heads, 64), jnp.float32),
                jnp.zeros((key_end, heads, 64), jnp.float32),
            )

        if number == 0:
            query_part, key_part, value_part = compute_back()
        else:
            query_part, key_part, value_part = lax.cond(start < count, compute_back, empty_back)
        query_blocks.append(query_part)
        key_total = key_total.at[:key_end].add(key_part)
        value_total = value_total.at[:key_end].add(value_part)
    query_total = jnp.concatenate(query_blocks, axis=0)
    qkv_grad = jnp.concatenate(
        [
            query_total.reshape(rows, width),
            key_total.reshape(rows, width),
            value_total.reshape(rows, width),
        ],
        axis=1,
    ).astype(jnp.bfloat16)
    in_grad = tr_matmul(normed1, qkv_grad)
    qkv_sums = jnp.sum(qkv_grad.astype(jnp.float32), axis=0)
    bias_in_grad = jnp.concatenate([qkv_sums[:width], qkv_sums[2 * width :]])
    normed1_grad = matmul_tr(qkv_grad, w_in_back)
    first_value, first_pull = jax.vjp(norm_rows, inputs, gain_first, shift_first)
    input_part, gain_one_grad, shift_one_grad = first_pull(normed1_grad)
    tokens_grad = (resid_grad + input_part).astype(jnp.bfloat16)
    mlp_grads = reduce_forward(
        gain_two_grad, shift_two_grad, up_grad, up_bias_grad, down_grad, down_bias_grad
    )
    attn_grads = reduce_attention(
        gain_one_grad, shift_one_grad, in_grad, bias_in_grad, out_grad, out_bias_grad
    )
    return (
        output[None],
        tokens_grad[None],
        attn_grads[0],
        attn_grads[1],
        attn_grads[2],
        attn_grads[3],
        attn_grads[4],
        attn_grads[5],
        mlp_grads[0],
        mlp_grads[1],
        mlp_grads[2],
        mlp_grads[3],
        mlp_grads[4],
        mlp_grads[5],
    )


def solution(mesh):
    placed = (
        P(("dp", "inner"), None, None),
        P(("dp", "inner")),
        P(("dp", "inner"), None, None),
        P(("dp", "inner")),
        P(("dp", "inner")),
        P(("dp", "inner"), None),
        P(("dp", "inner")),
        P(("dp", "inner"), None),
        P(("dp", "inner")),
        P(("dp", "inner")),
        P(("dp", "inner")),
        P(("dp", "inner"), None),
        P(("dp", "inner")),
        P(("dp", "inner"), None),
        P(("dp", "inner")),
    )
    return jax.shard_map(
        local,
        mesh=mesh,
        in_specs=placed,
        out_specs=(
            P(("dp", "inner"), None, None),
            P(("dp", "inner"), None, None),
            P(("dp", "inner")),
            P(("dp", "inner")),
            P(("dp", "inner"), None),
            P(("dp", "inner")),
            P(("dp", "inner"), None),
            P(("dp", "inner")),
            P(("dp", "inner")),
            P(("dp", "inner")),
            P(("dp", "inner"), None),
            P(("dp", "inner")),
            P(("dp", "inner"), None),
            P(("dp", "inner")),
        ),
        check_vma=False,
    )
```

profile of v0, /device:TPU:0, one launch (start us, length us, event | category | flops | bytes accessed | tf_op | source)
XLA Modules:
  0.0 844.8 jit_solution(8831942198419206770)
XLA Ops:
  17.5 42.7 %all-reduce.19 = (bf16[1536]{0:T(1024)(128)(2,1)S(1)}, bf16[768]{0:T(1024)(128)(2,1)}, bf16[768]{0:T(1024)(128)(2,1)S(1)}, bf16[768]{0:T(1024)(128)(2,1)S(1)}, b...) all-reduce(bf16[1536]{0:T(1024)(128)(2,1)S(1)} %dynamic-update-slic, ...), channel_id=1, replica_groups=mesh['dp'=8,'inner'=4] {'dp','inner'}, use_global_device_ids=true, to_apply=%add.4 | all-reduce | flops 9216 | bytes 36864
  60.2 1.7 copy.73
  63.7 1.6 copy.82
  65.8 7.8 all-gather.5.cloned.1.call-done
  73.6 6.4 add_convert_fusion
  80.1 1.5 fusion.73
  81.6 1.2 copy-done.17
  82.7 1.6 copy.80
  84.3 3.3 fusion.72
  88.0 1.7 copy.78
  89.7 2.6 copy.75
  92.3 2.3 copy.74
  94.6 2.6 copy.79
  97.1 36.9 %conditional.2 = (f32[12,512]{1,0:T(8,128)S(1)}, bf16[512,12,64]{0,2,1:T(8,128)(2,1)S(1)}) conditional(s32[]{:T(128)} %convert_element_type.126, () %tuple.50, (bf16[512,12,64]{0,2,1:T(8,128)(2,1)S(1)}, bf16[1024,12,64]{0,2,1:T(8,128)(2,1)}, bf16[1024,12,64]{0,2,1:T(8,128)(2,1)}, s32[]{:T(128)}) %tuple.106), branch_computations={%region_4.5_spmd, %region_5.8_spmd} | conditional | flops 1687416832 | bytes 189472848 | solution.py:188
  98.4 12.2 %fusion = (f32[12,512]{1,0:T(8,128)S(1)}, f32[12,512,1024]{2,1,0:T(8,128)}) fusion(pred[512,1024]{1,0:T(8,128)(4,1)S(1)} %iota_compare_fusion, bf16[512,12,64]{0,2,1:T(8,128)(2,1)S(1)} %get-tuple-element.86, bf16[1024,12,64]{0,2,1:T(8,128)(2,1)} %get-tuple-element.87), kind=kOutput, calls=%fused_computation.3 | convolution fusion | flops 824174592 | bytes 28073984 | tf_op jit(solution)/shard_map/cond/branch_1_fun/qhd,khd->hqk/dot_general | solution.py:87
  110.6 12.5 %fusion.1 = f32[12,512]{1,0:T(8,128)S(1)} fusion(f32[12,512,1024]{2,1,0:T(8,128)} %get-tuple-element.197, f32[12,512]{1,0:T(8,128)S(1)} %get-tuple-element.196, pred[512,1024]{1,0:T(8,128)(4,1)S(1)} %iota_compare_fusion), kind=kLoop, calls=%fused_computation.4 | loop fusion | flops 25159680 | bytes 25739264 | tf_op jit(solution)/shard_map/cond/branch_1_fun/reduce_sum | solution.py:99
  123.1 3.1 copy-done.1
  126.2 7.9 fusion.3
  135.0 3.2 fusion.28
  138.2 2.6 fusion.22
  140.8 1.9 copy-done
  142.7 4.0 fusion.54
  146.7 1.4 pad_maximum_fusion.1
  148.1 3.4 fusion.76
  151.5 1.6 copy-done.5
  154.2 40.5 %all-gather.9.cloned.1.call-done = bf16[768,3072]{1,0:T(8,128)(2,1)} async-done(((bf16[24,3072]{1,0:T(8,128)(2,1)}), bf16[768,3072]{1,0:T(8,128)(2,1)}) %all-gather.9.cloned.1.call-update) | async-done | bytes 4718608 | tf_op jit(solution)/shard_map/all_gather | solution.py:56
  194.7 11.0 %fusion.69 = f32[1024,3072]{1,0:T(8,128)} fusion(bf16[768,3072]{1,0:T(8,128)(2,1)} %all-gather.9.cloned.1.call-done, f32[1024,768]{0,1:T(8,128)} %copy-done.5, f32[768]{0:T(1024)S(1)} %convert_element_type.130, f32[768]{0:T(1024)S(1)} %convert_element_type.129, f32[1024]{0:T(1024)S(1)} %fusion.58, f32[1024]{0:T(1024)S(1)} %broadcast_multiply_fusion), kind=kOutput, calls=%fused_computation.126 | convolution fusion | flops 4835770368 | bytes 20461568 | tf_op jit(solution)/shard_map/dot_general | solution.py:26
  205.7 53.6 %all-gather.11.cloned.1.call-done = bf16[3072,768]{1,0:T(8,128)(2,1)} async-done(((bf16[96,768]{1,0:T(8,128)(2,1)}), bf16[3072,768]{1,0:T(8,128)(2,1)}) %all-gather.11.cloned.1.call-update) | async-done | bytes 4718608 | tf_op jit(solution)/shard_map/all_gather | solution.py:58
  259.3 18.1 %convert_reduce_fusion = (f32[3072]{0:T(1024)}, bf16[1024,3072]{1,0:T(8,128)(2,1)S(1)}) fusion(bf16[3072,768]{1,0:T(8,128)(2,1)} %all-gather.11.cloned.1.call-done, bf16[1,1024,768]{2,1,0:T(8,128)(2,1)S(1)} %copy-done.33, f32[1024,3072]{1,0:T(8,128)} %fusion.69, f32[3072]{0:T(1024)S(1)} %copy-done.54), kind=kOutput, calls=%fused_computation.38 | convolution fusion | flops 4916769792 | bytes 25190400 | tf_op jit(solution)/shard_map/dot_general | solution.py:30
  277.3 7.5 fusion.78
  284.8 3.7 copy.83
  288.5 3.5 multiply_reduce_fusion.2
  294.7 1.2 copy-done.37
  295.8 2.8 fusion.80
  298.7 3.2 fusion.48
  302.1 12.1 %multiply_reduce_fusion.1 = (f32[12,512]{1,0:T(8,128)S(1)}, f32[12,512,512]{1,2,0:T(8,128)}) fusion(f32[12,512]{1,0:T(8,128)S(1)} %log_add_fusion.1, f32[12,512,512]{1,2,0:T(8,128)} %copy-done, pred[512,512]{0,1:T(8,128)(4,1)S(1)} %iota_compare_fusion.2, bf16[512,12,64]{0,2,1:T(8,128)(2,1)S(1)} %bitcast.144, bf16[512,12,64]{0,2,1:T(8,128)(2,1)S(1)} %bitcast.143), kind=kOutput, calls=%fused_computation.40 | convolution fusion | flops 418375680 | bytes 27049984 | tf_op jit(solution)/shard_map/qhd,khd->hqk/dot_general | solution.py:115
  314.2 1.6 slice-done.2
  315.8 7.2 multiply_convert_fusion.3
  324.1 2.0 copy-done.2
  327.4 84.0 %conditional.3 = (f32[1024,12,64]{0,2,1:T(8,128)}, f32[1024,12,64]{0,2,1:T(8,128)}, bf16[512,12,64]{0,2,1:T(8,128)(2,1)S(1)}) conditional(s32[]{:T(128)} %convert_element_type.126, () %tuple.52, (bf16[512,12,64]{0,2,1:T(8,128)(2,1)S(1)}, bf16[1024,12,64]{0,2,1:T(8,128)(2,1)}, f32[12,512]{1,0:T(8,128)S(1)}, bf16[1024,768]{0,1:T(8,128)(2,1)S(1)}, ...), branch_computations={%region_13.14_spmd, %region_14.16_spmd} | conditional | flops 4122995200 | bytes 212725856 | solution.py:267
  327.9 12.0 %fusion.79 = f32[12,512,1024]{2,1,0:T(8,128)} fusion(bf16[512,12,64]{0,2,1:T(8,128)(2,1)S(1)} %get-tuple-element.90, bf16[1024,12,64]{0,2,1:T(8,128)(2,1)} %get-tuple-element.91), kind=kOutput, calls=%fused_computation.135 | convolution fusion | flops 805306368 | bytes 27525120 | tf_op jit(solution)/shard_map/cond/branch_1_fun/qhd,khd->hqk/dot_general | solution.py:87
  339.8 13.4 %fusion.10 = f32[1024,12,64]{0,2,1:T(8,128)} fusion(bf16[512,12,64]{0,2,1:T(8,128)(2,1)S(1)} %bitcast.146, f32[12,512,1024]{2,1,0:T(8,128)} %fusion.79, f32[12,512]{1,0:T(8,128)S(1)} %get-tuple-element.92, pred[512,1024]{1,0:T(8,128)(4,1)S(1)} %iota_compare_fusion.1), kind=kOutput, calls=%fused_computation.22 | convolution fusion | flops 830472192 | bytes 29646848 | tf_op jit(solution)/shard_map/cond/branch_1_fun/hqk,qhd->khd/dot_general | solution.py:112
  353.2 17.9 %multiply_reduce_fusion = (f32[12,512]{1,0:T(8,128)S(1)}, f32[12,512,1024]{2,1,0:T(8,128)}) fusion(f32[12,512,1024]{2,1,0:T(8,128)} %fusion.79, f32[12,512]{1,0:T(8,128)S(1)} %get-tuple-element.92, pred[512,1024]{1,0:T(8,128)(4,1)} %copy-done.23, bf16[512,12,64]{0,2,1:T(8,128)(2,1)} %bitcast.147, bf16[1024,12,64]{0,2,1:T(8,128)(2,1)S(1)} %get-tuple-element.94), kind=kOutput, calls=%fused_computation.15 | convolution fusion | flops 836757504 | bytes 53264384 | tf_op jit(solution)/shard_map/cond/branch_1_fun/qhd,khd->hqk/dot_general | solution.py:115
  371.1 22.7 %multiply_convert_fusion.1 = bf16[12,512,1024]{2,1,0:T(8,128)(2,1)} fusion(f32[12,512,1024]{2,1,0:T(8,128)} %get-tuple-element.199, f32[12,512,1024]{2,1,0:T(8,128)} %fusion.79, f32[12,512]{1,0:T(8,128)S(1)} %get-tuple-element.198, f32[12,512]{1,0:T(8,128)S(1)} %get-tuple-element.92, pred[512,1024]{1,0:T(8,128)(4,1)} %copy-done.23), kind=kLoop, calls=%fused_computation.14 | loop fusion | flops 37748736 | bytes 63488000 | tf_op jit(solution)/shard_map/cond/branch_1_fun/convert_element_type | solution.py:119
  393.8 8.9 %fusion.13 = bf16[512,12,64]{0,2,1:T(8,128)(2,1)S(1)} fusion(bf16[12,512,1024]{2,1,0:T(8,128)(2,1)} %multiply_convert_fusion.1, bf16[1024,12,64]{0,2,1:T(8,128)(2,1)} %get-tuple-element.91), kind=kOutput, calls=%fused_computation.24 | convolution fusion | flops 806092800 | bytes 14942208 | tf_op jit(solution)/shard_map/cond/branch_1_fun/hqk,khd->qhd/dot_general | solution.py:121
  402.7 8.5 %multiply_bitcast_fusion = f32[1024,12,64]{0,2,1:T(8,128)} fusion(bf16[512,12,64]{0,2,1:T(8,128)(2,1)S(1)} %get-tuple-element.90, bf16[12,512,1024]{2,1,0:T(8,128)(2,1)} %multiply_convert_fusion.1), kind=kOutput, calls=%fused_computation.20 | convolution fusion | flops 806092800 | bytes 16515072 | tf_op jit(solution)/shard_map/cond/branch_1_fun/hqk,qhd->khd/dot_general | solution.py:124
  412.5 5.4 multiply_bitcast_fusion.1
  417.9 6.2 fusion.50
  424.2 3.7 add_convert_fusion.2
  429.0 7.0 fusion.64
  436.2 13.3 %fusion.45 = f32[3072,768]{1,0:T(8,128)} fusion(bf16[1,1024,768]{2,1,0:T(8,128)(2,1)} %param.33, f32[1024,3072]{1,0:T(8,128)} %fusion.69, f32[3072]{0:T(1024)S(1)} %copy-done.54), kind=kOutput, calls=%fused_computation.89 | convolution fusion | flops 4863295488 | bytes 23605248 | tf_op jit(solution)/shard_map/dot_general | solution.py:36
  450.1 10.6 %fusion.68 = f32[768,3072]{1,0:T(8,128)} fusion(bf16[1024,3072]{1,0:T(8,128)(2,1)} %copy-done.61, f32[1024,768]{0,1:T(8,128)} %copy-done.5, f32[768]{0:T(1024)S(1)} %copy-done.39, f32[768]{0:T(1024)S(1)} %convert_element_type.129, f32[1024]{0:T(1024)S(1)} %fusion.58, f32[1024]{0:T(1024)S(1)} %broadcast_multiply_fusion), kind=kOutput, calls=%fused_computation.125 | convolution fusion | flops 4835770368 | bytes 18888704 | tf_op jit(solution)/shard_map/dot_general | solution.py:36
  461.4 12.3 %fusion.49 = bf16[1,1024,768]{1,2,0:T(8,128)(2,1)} fusion(f32[768]{0:T(1024)S(1)} %convert_element_type.134, f32[1024,768]{0,1:T(8,128)} %copy-done.5, bf16[3072,768]{1,0:T(8,128)(2,1)} %all-gather.11.cloned.1.call-done, f32[1024,3072]{1,0:T(8,128)} %fusion.69, f32[3072]{0:T(1024)S(1)} %copy-done.54), kind=kOutput, calls=%fused_computation.96 | convolution fusion | flops 4865654784 | bytes 22035456 | tf_op jit(solution)/shard_map/dot_general | solution.py:26
  473.8 2.6 copy.90
  476.4 8.5 %fusion.77 = (f32[768]{0:T(1024)S(1)}, f32[1024,768]{1,0:T(8,128)}) fusion(bf16[768,2304]{1,0:T(8,128)(2,1)} %all-gather.5.cloned.1.call-done, bf16[1024,768]{0,1:T(8,128)(2,1)S(1)} %bitcast.134, bf16[1024,768]{0,1:T(8,128)(2,1)} %bitcast.137, bf16[1024,768]{0,1:T(8,128)(2,1)} %bitcast.140), kind=kOutput, calls=%fused_computation.133 | convolution fusion | flops 3638820096 | bytes 11406336 | tf_op jit(solution)/shard_map/dot_general | solution.py:30
  484.8 4.5 copy.87
  489.3 2.6 convert_reduce_fusion.1
  492.8 1.3 fusion.39
  495.1 1.7 convert_reduce_fusion.2
  496.9 39.6 %all-reduce.18 = (f32[768]{0:T(1024)S(1)}, f32[768]{0:T(1024)S(1)}, f32[1536]{0:T(1024)S(1)}, f32[768]{0:T(1024)S(1)}, f32[768]{0:T(1024)S(1)}, /*index=5*/f32[7...) all-reduce(f32[768]{0:T(1024)S(1)} %get-tuple-element.174, ...), channel_id=2, replica_groups=mesh['dp'=8,'inner'=4] {'dp','inner'}, use_global_device_ids=true, to_apply=%region_19.20.clone | all-reduce | flops 9216 | bytes 73728
  540.0 1.6 copy.91
  542.8 11.4 %reduce-scatter.5.cloned.1.call-done = f32[24,2304]{1,0:T(8,128)} async-done(((f32[768,2304]{1,0:T(8,128)}), f32[24,2304]{1,0:T(8,128)}) %reduce-scatter.5.cloned.1.call-update) | async-done | bytes 221200 | tf_op jit(solution)/shard_map/reduce_scatter | solution.py:78
  554.2 141.6 %reduce-scatter.11.cloned.1.call-done = f32[96,768]{1,0:T(8,128)} async-done(((f32[3072,768]{1,0:T(8,128)}), f32[96,768]{1,0:T(8,128)}) %reduce-scatter.11.cloned.1.call-update) | async-done | bytes 294928 | tf_op jit(solution)/shard_map/reduce_scatter | solution.py:69
  695.8 141.9 %reduce-scatter.9.cloned.1.call-done = f32[24,3072]{1,0:T(8,128)} async-done(((f32[768,3072]{1,0:T(8,128)}), f32[24,3072]{1,0:T(8,128)}) %reduce-scatter.9.cloned.1.call-update) | async-done | bytes 294928 | tf_op jit(solution)/shard_map/reduce_scatter | solution.py:67
  (207 shorter events, 30.6 us)
Async XLA Ops:
  7.2 56.5 %copy-start.32 = (bf16[1,1024,768]{2,1,0:T(8,128)(2,1)S(1)}, bf16[1,1024,768]{2,1,0:T(8,128)(2,1)}, u32[]{:S(2)}) copy-start(bf16[1,1024,768]{2,1,0:T(8,128)(2,1)} %param.33) | copy-start | bytes 4718596
  7.2 66.4 %all-gather.5.cloned.1.call-start = ((), (), s32[]{:S(2)}) async-start(), calls=%async_computation.4 | async-start | bytes 3649536 | tf_op jit(solution)/shard_map/all_gather | solution.py:45
  7.9 140.2 %all-gather.7.cloned.1.call-start = ((), (), s32[]{:S(2)}) async-start(), calls=%async_computation.5 | async-start | bytes 1216512 | tf_op jit(solution)/shard_map/all_gather | solution.py:47
  8.7 186.0 %all-gather.9.cloned.1.call-start = ((), (), s32[]{:S(2)}) async-start(), calls=%async_computation.6 | async-start | bytes 4866048 | tf_op jit(solution)/shard_map/all_gather | solution.py:56
  9.4 249.9 %all-gather.11.cloned.1.call-start = ((), (), s32[]{:S(2)}) async-start(), calls=%async_computation.7 | async-start | bytes 4866048 | tf_op jit(solution)/shard_map/all_gather | solution.py:58
  10.0 532.8 %reduce-scatter.7.cloned.1.call-start = ((), (), s32[]{:S(2)}) async-start(), calls=%async_computation.9 | async-start | bytes 2433024 | tf_op jit(solution)/shard_map/reduce_scatter | solution.py:80
  62.0 86.1 %copy-start.3 = (bf16[1,1024,768]{1,2,0:T(8,128)(2,1)}, bf16[1,1024,768]{1,2,0:T(8,128)(2,1)S(1)}, u32[]{:S(2)}) copy-start(bf16[1,1024,768]{1,2,0:T(8,128)(2,1)S(1)} %copy.73) | copy-start | bytes 4718596
  63.0 17.0 %copy-start.42 = (f32[768]{0:T(1024)}, f32[768]{0:T(1024)S(1)}, u32[]{:S(2)}) copy-start(f32[768]{0:T(1024)S(1)} %convert_element_type.119) | copy-start | bytes 9220
  63.0 17.0 %copy-start.56 = (f32[768]{0:T(1024)}, f32[768]{0:T(1024)S(1)}, u32[]{:S(2)}) copy-start(f32[768]{0:T(1024)S(1)} %convert_element_type.120) | copy-start | bytes 9220
  63.1 131.6 %copy-start.38 = (f32[768]{0:T(1024)}, f32[768]{0:T(1024)S(1)}, u32[]{:S(2)}) copy-start(f32[768]{0:T(1024)S(1)} %convert_element_type.130) | copy-start | bytes 9220
  65.3 14.7 %copy-start.40 = (f32[1024]{0:T(1024)}, f32[1024]{0:T(1024)S(1)}, u32[]{:S(2)}) copy-start(f32[1024]{0:T(1024)S(1)} %broadcast_multiply_fusion.1) | copy-start | bytes 12292
  65.8 7.8 copy-start.48
  65.8 7.8 copy-start.44
  80.1 2.7 copy-start.17
  87.9 47.0 %copy-start.15 = (bf16[512,768]{0,1:T(8,128)(2,1)}, bf16[512,768]{0,1:T(8,128)(2,1)S(1)}, u32[]{:S(2)}) copy-start(bf16[512,768]{0,1:T(8,128)(2,1)S(1)} %copy.76) | copy-start | bytes 2359300
  89.7 7.5 copy-start.11
  98.4 24.7 %copy-start.20 = (bf16[1024,12,64]{0,2,1:T(8,128)(2,1)S(1)}, bf16[1024,12,64]{0,2,1:T(8,128)(2,1)}, u32[]{:S(2)}) copy-start(bf16[1024,12,64]{0,2,1:T(8,128)(2,1)} %get-tuple-element.88) | copy-start | bytes 4718596 | tf_op jit(solution)/shard_map/cond
  110.6 15.6 %copy-start.1 = (f32[12,512,1024]{2,1,0:T(8,128)S(1)}, f32[12,512,1024]{2,1,0:T(8,128)}, u32[]{:S(2)}) copy-start(f32[12,512,1024]{2,1,0:T(8,128)} %get-tuple-element.197) | copy-start | bytes 75497472 | tf_op jit(solution)/shard_map/cond
  138.2 4.5 copy-start
  138.2 4.5 copy-start.25
  142.7 4.0 copy-start.30
  151.5 1.6 copy-start.5
  154.1 105.1 %copy-start.33 = (bf16[1,1024,768]{2,1,0:T(8,128)(2,1)S(1)}, bf16[1,1024,768]{2,1,0:T(8,128)(2,1)}, u32[]{:S(2)}) copy-start(bf16[1,1024,768]{2,1,0:T(8,128)(2,1)} %param.33) | copy-start | bytes 4718596
  154.2 105.1 %copy-start.54 = (f32[3072]{0:T(1024)S(1)}, f32[3072]{0:T(1024)}, u32[]{:S(2)}) copy-start(f32[3072]{0:T(1024)} %convert_element_type.132) | copy-start | bytes 36868
  259.3 18.1 %copy-start.24 = (bf16[768,3072]{1,0:T(8,128)(2,1)S(1)}, bf16[768,3072]{1,0:T(8,128)(2,1)}, u32[]{:S(2)}) copy-start(bf16[768,3072]{1,0:T(8,128)(2,1)} %all-gather.9.cloned.1.call-done) | copy-start | bytes 14155780
  277.3 7.5 copy-start.61
  284.8 3.7 copy-start.6
  288.5 3.5 copy-start.51
  288.5 3.5 copy-start.10
  292.9 1.7 copy-start.8
  293.0 1.7 copy-start.46
  293.5 2.4 copy-start.36
  295.8 2.9 copy-start.60
  298.7 3.4 copy-start.26
  298.7 255.5 %reduce-scatter.5.cloned.1.call-start = ((), (), s32[]{:S(2)}) async-start(), calls=%async_computation.8 | async-start | bytes 7299072 | tf_op jit(solution)/shard_map/reduce_scatter | solution.py:78
  301.9 12.2 %copy-start.34 = (bf16[1024,768]{0,1:T(8,128)(2,1)}, bf16[1024,768]{0,1:T(8,128)(2,1)S(1)}, u32[]{:S(2)}) copy-start(bf16[1024,768]{0,1:T(8,128)(2,1)S(1)} %fusion.48) | copy-start | bytes 4718596
  302.0 12.1 %copy-start.27 = (bf16[512,768]{0,1:T(8,128)(2,1)}, bf16[512,768]{0,1:T(8,128)(2,1)S(1)}, u32[]{:S(2)}) copy-start(bf16[512,768]{0,1:T(8,128)(2,1)S(1)} %slice.168) | copy-start | bytes 2359300
  302.0 12.1 %slice-start = ((s8[12582912]{0:T(1024)(128)(4,1)}), s8[4194304]{0:T(1024)(128)(4,1)S(1)}, s32[]{:S(2)}) async-start(s8[12582912]{0:T(1024)(128)(4,1)} %bitcast.123), calls=%async_computation.12 | async-start | bytes 8388608
  302.1 12.1 %slice-start.1 = ((s8[12582912]{0:T(1024)(128)(4,1)}), s8[4194304]{0:T(1024)(128)(4,1)S(1)}, s32[]{:S(2)}) async-start(s8[12582912]{0:T(1024)(128)(4,1)} %bitcast.123), calls=%async_computation.13 | async-start | bytes 8388608
  302.1 13.7 %slice-start.2 = ((s8[12582912]{0:T(1024)(128)(4,1)}), s8[4194304]{0:T(1024)(128)(4,1)S(1)}, s32[]{:S(2)}) async-start(s8[12582912]{0:T(1024)(128)(4,1)} %bitcast.123), calls=%async_computation.14 | async-start | bytes 8388608
  315.8 7.2 copy-start.16
  322.9 3.2 copy-start.2
  322.9 3.2 copy-start.12
  323.0 3.5 copy-start.19
  323.0 4.4 copy-start.35
  327.5 12.4 %copy-start.31 = (bf16[512,768]{0,1:T(8,128)(2,1)}, bf16[512,768]{0,1:T(8,128)(2,1)S(1)}, u32[]{:S(2)}) copy-start(bf16[512,768]{0,1:T(8,128)(2,1)S(1)} %slice.126) | copy-start | bytes 2359300 | tf_op jit(solution)/shard_map/cond
  327.9 12.0 %copy-start.23 = (pred[512,1024]{1,0:T(8,128)(4,1)}, pred[512,1024]{1,0:T(8,128)(4,1)S(1)}, u32[]{:S(2)}) copy-start(pred[512,1024]{1,0:T(8,128)(4,1)S(1)} %iota_compare_fusion.1) | copy-start | bytes 1572868 | tf_op jit(solution)/shard_map/cond
  412.5 15.4 %copy-start.22 = (bf16[1024,12,64]{0,2,1:T(8,128)(2,1)}, bf16[1024,12,64]{0,2,1:T(8,128)(2,1)S(1)}, u32[]{:S(2)}) copy-start(bf16[1024,12,64]{0,2,1:T(8,128)(2,1)S(1)} %pad_maximum_fusion.2) | copy-start | bytes 4718596
  412.5 5.4 copy-start.28
  424.1 4.9 copy-start.4
  424.1 4.9 copy-start.41
  424.1 4.9 copy-start.43
  424.1 4.9 copy-start.45
  424.1 4.9 copy-start.57
  436.1 259.7 %reduce-scatter.11.cloned.1.call-start = ((), (), s32[]{:S(2)}) async-start(), calls=%async_computation.11 | async-start | bytes 9732096 | tf_op jit(solution)/shard_map/reduce_scatter | solution.py:69
  449.5 388.2 %reduce-scatter.9.cloned.1.call-start = ((), (), s32[]{:S(2)}) async-start(), calls=%async_computation.10 | async-start | bytes 9732096 | tf_op jit(solution)/shard_map/reduce_scatter | solution.py:67
  489.3 2.8 copy-start.7
  492.7 1.9 copy-start.9
  492.7 2.4 copy-start.14
  492.7 2.4 copy-start.47
  495.1 1.7 copy-start.52
  495.1 1.8 copy-start.53
  495.1 1.8 copy-start.55
  495.1 1.8 copy-start.58
  (9 other events, 8.4 us)
Sparse Core Ops, SparseCore 0:
  10.8 62.7 all-gather.4
  76.4 52.8 all-gather.6
  132.1 62.5 all-gather.8
  197.3 61.8 all-gather.10
  298.8 97.9 reduce-scatter.6
  436.2 117.8 reduce-scatter.4
  560.6 135.0 reduce-scatter.10
  702.3 135.3 reduce-scatter.8
where the time goes:
time: 852 us; the launch traced here: 845 us
  waiting for transfers between devices  399 us (47%)
  matrix products  217 us (25%)
  blocking collectives  82.3 us (10%)
  other arithmetic  66 us (8%)
  local copies, waits for them, and re-layouts  63.4 us (7%)
  between operations  15.8 us (2%)
    reduce_scatter x1, waiting for transfers between devices, reduce_forward(): lax.psum_scatter(up_grad, ('dp', 'inner'), scatter_dimension=0, tiled=True)  142 us
    reduce_scatter x1, waiting for transfers between devices, reduce_forward(): lax.psum_scatter(down_grad, ('dp', 'inner'), scatter_dimension=0, tiled=T...  142 us
    unnamed x2, blocking collectives  82.3 us
    all_gather x1, waiting for transfers between devices, fetch_forward(): lax.all_gather(w_down, ('dp', 'inner'), axis=0, tiled=True)  53.6 us
    all_gather x1, waiting for transfers between devices, fetch_forward(): lax.all_gather(w_up, ('dp', 'inner'), axis=0, tiled=True)  40.5 us
    dot_general x4, matrix products, matmul_tr(): lax.dot_general(left, right, (((1,), (1,)), ((), ())), preferred_element_...  37.2 us
    unnamed x150, local copies, waits for them, and re-layouts  36.1 us
    dot_general x4, matrix products, tr_matmul(): lax.dot_general(left, right, (((0,), (0,)), ((), ())), preferred_element_...  33.8 us
  transfers between devices with their start and end apart: 8, of which 6 were waited for; matrix products, arithmetic and copies ran while one was open for 34% of the time, Pallas kernels for 0%

commit v1 on v0

v1 whole, which is shorter than its diff:
```python
import functools

import jax
import jax.numpy as jnp
from jax import lax
from jax.experimental import pallas as pl
from jax.experimental.pallas import tpu as pltpu
from jax.sharding import PartitionSpec as P

EPSILON = 1e-05
SCALE = 0.125
MASKED = -1000000000.0
AXES = ("dp", "inner")
HEAD = 64
PAIR = 2 * HEAD


def norm_stats(values):
    centre = values - jnp.mean(values, axis=-1, keepdims=True)
    spread = jnp.mean(centre * centre, axis=-1, keepdims=True)
    inverse = lax.rsqrt(spread + EPSILON)
    return centre * inverse, inverse


def norm_back(grad, xhat, inverse, gain):
    scaled = grad * gain
    first = jnp.mean(scaled, axis=-1, keepdims=True)
    second = jnp.mean(scaled * xhat, axis=-1, keepdims=True)
    return inverse * (scaled - first - xhat * second)


def gelu_both(values):
    inner = 0.7978845608028654 * (values + 0.044715 * values * values * values)
    bent = jnp.tanh(inner)
    half = 0.5 * (1.0 + bent)
    slope = half + 0.5 * values * (1.0 - bent * bent) * (
        0.7978845608028654 * (1.0 + 3.0 * 0.044715 * values * values)
    )
    return values * half, slope


def matmul(left, right):
    return jnp.dot(left, right, preferred_element_type=jnp.float32)


def matmul_tr(left, right):
    return lax.dot_general(
        left, right, (((1,), (1,)), ((), ())), preferred_element_type=jnp.float32
    )


def tr_matmul(left, right):
    return lax.dot_general(
        left, right, (((0,), (0,)), ((), ())), preferred_element_type=jnp.float32
    )


class Net:
    def __init__(self, dp, inner):
        self.count = dp * inner
        self.inner = inner
        self.rest = dp // 2
        self.inner_bits = [1 << b for b in range(inner.bit_length() - 1)]
        self.rest_bits = [1 << b for b in range(self.rest.bit_length() - 1)]
        place = lax.axis_index("dp")
        self.at_inner = lax.axis_index("inner")
        self.at_core = place % 2
        self.at_rest = place // 2

    def swap(self, value, mask):
        return lax.ppermute(value, AXES, [(i, i ^ mask) for i in range(self.count)])

    def swap_inner(self, value, bit):
        return self.swap(value, bit)

    def swap_core(self, value):
        return self.swap(value, self.inner)

    def swap_rest(self, value, bit):
        return self.swap(value, bit * self.inner * 2)

    def order(self, color):
        return self.rest_bits if color == 0 else self.rest_bits[::-1]

    def slot(self, rel, color):
        out = 0
        for at, bit in enumerate(self.order(color)):
            out = out + (((rel // bit) % 2) << at)
        return out

    def gather_inner(self, shards):
        rows = [shard[None] for shard in shards]
        for bit in self.inner_bits[::-1]:
            rows = [jnp.concatenate([x, self.swap_inner(x, bit)], axis=0) for x in rows]
        places = []
        for z in range(self.inner):
            rel = self.at_inner ^ z
            flat = 0
            for at, bit in enumerate(self.inner_bits[::-1]):
                flat = flat + (((rel // bit) % 2) << at)
            places.append(flat)
        return [
            jnp.concatenate(
                [lax.dynamic_index_in_dim(x, flat, 0, keepdims=False) for flat in places], axis=0
            )[None]
            for x in rows
        ]

    def gather_rest(self, groups, colors):
        for step in range(len(self.rest_bits)):
            groups = [
                jnp.concatenate([x, self.swap_rest(x, self.order(c)[step])], axis=0)
                for x, c in zip(groups, colors)
            ]
        return groups

    def gather(self, shards, colors):
        groups = self.gather_rest(self.gather_inner(shards), colors)
        return [(x, self.swap_core(x)) for x in groups]

    def assemble(self, pair, color):
        own, other = pair
        both = jnp.concatenate([own, other], axis=0)
        blocks = []
        for rest in range(self.rest):
            for core in range(2):
                flat = (self.at_core ^ core) * self.rest + self.slot(self.at_rest ^ rest, color)
                blocks.append(lax.dynamic_index_in_dim(both, flat, 0, keepdims=False))
        return jnp.concatenate(blocks, axis=0)

    def split(self, grad, color):
        rows, cols = grad.shape
        view = grad.astype(jnp.bfloat16).reshape(self.rest, 2, rows // (2 * self.rest), cols)
        halves = []
        for core in (self.at_core, 1 - self.at_core):
            half = lax.dynamic_index_in_dim(view, core, 1, keepdims=False)
            blocks = [None] * self.rest
            for rel in range(self.rest):
                blocks[self.slot(rel, color)] = lax.dynamic_index_in_dim(
                    half, self.at_rest ^ rel, 0, keepdims=True
                )
            halves.append(jnp.concatenate(blocks, axis=0))
        return halves

    def scatter(self, halves, colors):
        def add(a, b):
            return (a.astype(jnp.float32) + b.astype(jnp.float32)).astype(jnp.bfloat16)

        sums = []
        for keep, send in halves:
            recv = self.swap_core(send)
            n = keep.shape[0] // 2
            sums.append((add(keep[:n], recv[:n]), add(keep[n:], recv[n:])))
        steps = len(self.rest_bits)
        for step in range(steps):
            following = []
            for (keep, send), c in zip(sums, colors):
                recv = self.swap_rest(send, self.order(c)[steps - 1 - step])
                if step < steps - 1:
                    n = keep.shape[0] // 2
                    following.append((add(keep[:n], recv[:n]), add(keep[n:], recv[n:])))
                else:
                    following.append(add(keep, recv))
            sums = following
        out = []
        for x in sums:
            rows = x.shape[1] // self.inner
            view = x.reshape(self.inner, rows, x.shape[2])
            total = lax.dynamic_index_in_dim(view, self.at_inner, 0, keepdims=False).astype(
                jnp.float32
            )
            for mask in range(1, self.inner):
                send = lax.dynamic_index_in_dim(view, self.at_inner ^ mask, 0, keepdims=False)
                total = total + self.swap(send, mask).astype(jnp.float32)
            out.append(total)
        return out


def attention_forward_kernel(step, count_ref, q_ref, k_ref, v_ref, mixed_ref, log_ref):
    rows = q_ref.shape[0]
    count = count_ref[0]
    for head in range(2):
        cols = slice(head * HEAD, (head + 1) * HEAD)
        turned = jnp.transpose(v_ref[:, cols].astype(jnp.float32)).astype(jnp.bfloat16)
        for start in range(0, rows, step):
            end = start + step

            def block():
                query = q_ref[start:end, cols] * jnp.bfloat16(SCALE)
                scores = matmul_tr(k_ref[0:end, cols], query)
                keys_at = lax.broadcasted_iota(jnp.int32, (step, step), 0)
                rows_at = lax.broadcasted_iota(jnp.int32, (step, step), 1)
                last = jnp.where(keys_at <= rows_at, scores[start:end], MASKED)
                scores = jnp.concatenate([scores[:start], last], axis=0) if start else last
                top = jnp.max(scores, axis=0, keepdims=True)
                expo = jnp.exp(scores - top)
                total = jnp.sum(expo, axis=0, keepdims=True)
                out = matmul(turned[:, 0:end], expo.astype(jnp.bfloat16)) / total
                live = lax.broadcasted_iota(jnp.int32, (1, step), 1) + start < count
                out = jnp.where(live, out, 0.0)
                mixed_ref[start:end, cols] = jnp.transpose(out).astype(jnp.bfloat16)
                log_ref[0, head : head + 1, start:end] = top + jnp.log(total)

            def empty():
                mixed_ref[start:end, cols] = jnp.zeros((step, HEAD), jnp.bfloat16)
                log_ref[0, head : head + 1, start:end] = jnp.zeros((1, step), jnp.float32)

            if start == 0:
                block()
            else:
                pl.when(start < count)(block)
                pl.when(start >= count)(empty)


def attention_forward(qkv, count, first, pairs):
    rows, wide = qkv.shape
    total = wide // (3 * PAIR)
    step = min(256, rows)
    return pl.pallas_call(
        functools.partial(attention_forward_kernel, step),
        grid_spec=pltpu.PrefetchScalarGridSpec(
            num_scalar_prefetch=1,
            grid=(pairs,),
            in_specs=[
                pl.BlockSpec((rows, PAIR), lambda i, n: (0, first + i)),
                pl.BlockSpec((rows, PAIR), lambda i, n: (0, total + first + i)),
                pl.BlockSpec((rows, PAIR), lambda i, n: (0, 2 * total + first + i)),
            ],
            out_specs=[
                pl.BlockSpec((rows, PAIR), lambda i, n: (0, i)),
                pl.BlockSpec((1, 2, rows), lambda i, n: (i, 0, 0)),
            ],
        ),
        out_shape=[
            jax.ShapeDtypeStruct((rows, pairs * PAIR), jnp.bfloat16),
            jax.ShapeDtypeStruct((pairs, 2, rows), jnp.float32),
        ],
        cost_estimate=pl.CostEstimate(
            flops=pairs * 2 * rows * rows * 256 * 2,
            bytes_accessed=pairs * rows * PAIR * 8,
            transcendentals=pairs * rows * rows,
        ),
        name="attention_forward",
    )(count, qkv, qkv, qkv)


def attention_backward_kernel(
    step,
    count_ref,
    q_ref,
    k_ref,
    v_ref,
    mixed_ref,
    grad_ref,
    log_ref,
    dq_ref,
    dk_ref,
    dv_ref,
    dk_acc,
    dv_acc,
):
    rows = q_ref.shape[0]
    count = count_ref[0]
    prod = grad_ref[...].astype(jnp.float32) * mixed_ref[...].astype(jnp.float32)
    prod = jnp.transpose(prod)
    for head in range(2):
        cols = slice(head * HEAD, (head + 1) * HEAD)
        inner = jnp.sum(prod[cols], axis=0, keepdims=True)
        turned = jnp.transpose(k_ref[:, cols].astype(jnp.float32)).astype(jnp.bfloat16)
        dk_acc[...] = jnp.zeros_like(dk_acc)
        dv_acc[...] = jnp.zeros_like(dv_acc)
        for start in range(0, rows, step):
            end = start + step

            def block():
                query = q_ref[start:end, cols] * jnp.bfloat16(SCALE)
                grad = grad_ref[start:end, cols]
                scores = matmul_tr(k_ref[0:end, cols], query)
                probs = jnp.exp(scores - log_ref[0, head : head + 1, start:end])
                keys_at = lax.broadcasted_iota(jnp.int32, (step, step), 0)
                rows_at = lax.broadcasted_iota(jnp.int32, (step, step), 1)
                last = jnp.where(keys_at <= rows_at, probs[start:end], 0.0)
                probs = jnp.concatenate([probs[:start], last], axis=0) if start else last
                dv_acc[0:end] += matmul(probs.astype(jnp.bfloat16), grad)
                dprobs = matmul_tr(v_ref[0:end, cols], grad)
                dscores = (probs * (dprobs - inner[:, start:end])).astype(jnp.bfloat16)
                dk_acc[0:end] += matmul(dscores, query)
                dq = matmul(turned[:, 0:end], dscores) * SCALE
                dq_ref[start:end, cols] = jnp.transpose(dq).astype(jnp.bfloat16)

            def empty():
                dq_ref[start:end, cols] = jnp.zeros((step, HEAD), jnp.bfloat16)

            if start == 0:
                block()
            else:
                pl.when(start < count)(block)
                pl.when(start >= count)(empty)
        dk_ref[:, cols] = dk_acc[...].astype(jnp.bfloat16)
        dv_ref[:, cols] = dv_acc[...].astype(jnp.bfloat16)


def attention_backward(qkv, mixed, grad, logs, count, first, pairs):
    rows, wide = qkv.shape
    total = wide // (3 * PAIR)
    step = min(256, rows)
    part = jax.ShapeDtypeStruct((rows, pairs * PAIR), jnp.bfloat16)
    return pl.pallas_call(
        functools.partial(attention_backward_kernel, step),
        grid_spec=pltpu.PrefetchScalarGridSpec(
            num_scalar_prefetch=1,
            grid=(pairs,),
            in_specs=[
                pl.BlockSpec((rows, PAIR), lambda i, n: (0, first + i)),
                pl.BlockSpec((rows, PAIR), lambda i, n: (0, total + first + i)),
                pl.BlockSpec((rows, PAIR), lambda i, n: (0, 2 * total + first + i)),
                pl.BlockSpec((rows, PAIR), lambda i, n: (0, i)),
                pl.BlockSpec((rows, PAIR), lambda i, n: (0, first + i)),
                pl.BlockSpec((1, 2, rows), lambda i, n: (i, 0, 0)),
            ],
            out_specs=[pl.BlockSpec((rows, PAIR), lambda i, n: (0, i))] * 3,
            scratch_shapes=[pltpu.VMEM((rows, HEAD), jnp.float32)] * 2,
        ),
        out_shape=[part] * 3,
        cost_estimate=pl.CostEstimate(
            flops=pairs * 2 * rows * rows * 256 * 5,
            bytes_accessed=pairs * rows * PAIR * 16,
            transcendentals=pairs * rows * rows,
        ),
        name="attention_backward",
    )(count, qkv, qkv, qkv, mixed, grad, logs)


def local(
    dp,
    inner,
    tokens,
    lengths,
    cotangent,
    norm1_gain,
    norm1_bias,
    attn_in,
    attn_bias,
    attn_out,
    out_bias,
    norm2_gain,
    norm2_bias,
    mlp_up,
    up_bias,
    mlp_down,
    down_bias,
):
    net = Net(dp, inner)
    n = net.count
    tok = tokens[0]
    grad_out = cotangent[0]
    rows, width = tok.shape
    wide = mlp_up.shape[1]
    r = attn_in.shape[0]
    places = jnp.arange(rows, dtype=jnp.int32)
    count = lengths[0]

    small = jnp.concatenate(
        [norm1_gain, norm1_bias, attn_bias, out_bias, norm2_gain, norm2_bias, up_bias, down_bias]
    )
    sizes = [r, r, 2 * r, r, r, r, up_bias.shape[0], r]
    padded = -(-small.shape[0] // 128) * 128
    small = jnp.pad(small, (0, padded - small.shape[0]))[None]

    half = 3 * width // 2
    in_a, in_b, small_all = net.gather(
        [attn_in[:, :half], attn_in[:, half:], small], [0, 1, 0]
    )
    w_in = jnp.concatenate([net.assemble(in_a, 0), net.assemble(in_b, 1)], axis=1)
    small_all = net.assemble(small_all, 0)
    pieces = []
    at = 0
    for size in sizes:
        pieces.append(small_all[:, at : at + size].reshape(-1).astype(jnp.float32))
        at += size
    gain_one, shift_one, bias_in, bias_out, gain_two, shift_two, bias_up, bias_down = pieces

    out_a, out_b, down, up = net.gather(
        [attn_out[:, : width // 2], attn_out[:, width // 2 :], mlp_down, mlp_up], [0, 1, 0, 1]
    )
    w_out = jnp.concatenate([net.assemble(out_a, 0), net.assemble(out_b, 1)], axis=1)
    w_up = net.assemble(up, 1)
    w_down = net.assemble(down, 0)

    inputs = tok.astype(jnp.float32)
    xhat1, inverse1 = norm_stats(inputs)
    normed1 = (xhat1 * gain_one + shift_one).astype(jnp.bfloat16)
    full_bias = jnp.concatenate([bias_in[:width], jnp.zeros((width,), jnp.float32), bias_in[width:]])
    qkv = (matmul(normed1, w_in) + full_bias).astype(jnp.bfloat16)
    pairs = width // PAIR
    groups = 3 if pairs % 3 == 0 else 1
    each = pairs // groups
    mixed_parts = []
    log_parts = []
    for g in range(groups):
        part, logs = attention_forward(qkv, lengths, g * each, each)
        mixed_parts.append(part)
        log_parts.append(logs)
    mixed = jnp.concatenate(mixed_parts, axis=1)
    resid = inputs + matmul(mixed, w_out) + bias_out
    xhat2, inverse2 = norm_stats(resid)
    normed2 = (xhat2 * gain_two + shift_two).astype(jnp.bfloat16)
    hidden = matmul(normed2, w_up) + bias_up
    act_float, slope = gelu_both(hidden)
    activated = act_float.astype(jnp.bfloat16)
    output = (resid + matmul(activated, w_down) + bias_down).astype(jnp.bfloat16)

    grad_float = grad_out.astype(jnp.float32)
    down_grad = tr_matmul(activated, grad_out)
    down_bias_grad = jnp.sum(grad_float, axis=0)
    hidden_grad = (matmul_tr(grad_out, w_down) * slope).astype(jnp.bfloat16)
    up_grad = tr_matmul(normed2, hidden_grad)
    up_bias_grad = jnp.sum(hidden_grad.astype(jnp.float32), axis=0)
    down_sum, up_sum = net.scatter(
        [net.split(down_grad, 0), net.split(up_grad, 1)], [0, 1]
    )
    normed2_grad = matmul_tr(hidden_grad, w_up)
    gain_two_grad = jnp.sum(normed2_grad * xhat2, axis=0)
    shift_two_grad = jnp.sum(normed2_grad, axis=0)
    resid_grad = grad_float + norm_back(normed2_grad, xhat2, inverse2, gain_two)
    resid_low = resid_grad.astype(jnp.bfloat16)
    out_grad = tr_matmul(mixed, resid_low)
    out_bias_grad = jnp.sum(resid_low.astype(jnp.float32), axis=0)
    live = (places < count).astype(jnp.float32)[:, None]
    mixed_grad = (matmul_tr(resid_low, w_out) * live).astype(jnp.bfloat16)
    dq, dk, dv = [], [], []
    for g in range(groups):
        parts = attention_backward(
            qkv, mixed_parts[g], mixed_grad, log_parts[g], lengths, g * each, each
        )
        dq.append(parts[0])
        dk.append(parts[1])
        dv.append(parts[2])
    qkv_grad = jnp.concatenate(dq + dk + dv, axis=1)
    in_grad = tr_matmul(normed1, qkv_grad)
    qkv_sums = jnp.sum(qkv_grad.astype(jnp.float32), axis=0)
    bias_in_grad = jnp.concatenate([qkv_sums[:width], qkv_sums[2 * width :]])
    normed1_grad = matmul_tr(qkv_grad, w_in)
    gain_one_grad = jnp.sum(normed1_grad * xhat1, axis=0)
    shift_one_grad = jnp.sum(normed1_grad, axis=0)
    tokens_grad = (resid_grad + norm_back(normed1_grad, xhat1, inverse1, gain_one)).astype(
        jnp.bfloat16
    )
    small_grads = [
        gain_one_grad,
        shift_one_grad,
        bias_in_grad,
        out_bias_grad,
        gain_two_grad,
        shift_two_grad,
        up_bias_grad,
        down_bias_grad,
    ]
    small_grad = jnp.concatenate([g.reshape(n, -1) for g in small_grads], axis=1)
    small_grad = jnp.pad(small_grad, ((0, 0), (0, padded - small_grad.shape[1])))
    in_sum_a, in_sum_b, out_sum, small_sum = net.scatter(
        [
            net.split(in_grad[:, :half], 0),
            net.split(in_grad[:, half:], 1),
            net.split(out_grad, 0),
            net.split(small_grad, 1),
        ],
        [0, 1, 0, 1],
    )
    in_sum = jnp.concatenate([in_sum_a, in_sum_b], axis=1)
    outs = []
    at = 0
    for size in sizes:
        outs.append(small_sum[0, at : at + size])
        at += size
    return (
        output[None],
        tokens_grad[None],
        outs[0],
        outs[1],
        in_sum,
        outs[2],
        out_sum,
        outs[3],
        outs[4],
        outs[5],
        up_sum,
        outs[6],
        down_sum,
        outs[7],
    )


def solution(mesh):
    rows = P(AXES)
    flat = P(AXES, None)
    deep = P(AXES, None, None)
    return jax.shard_map(
        functools.partial(local, mesh.shape["dp"], mesh.shape["inner"]),
        mesh=mesh,
        in_specs=(
            deep,
            rows,
            deep,
            rows,
            rows,
            flat,
            rows,
            flat,
            rows,
            rows,
            rows,
            flat,
            rows,
            flat,
            rows,
        ),
        out_specs=(
            deep,
            deep,
            rows,
            rows,
            flat,
            rows,
            flat,
            rows,
            rows,
            rows,
            flat,
            rows,
            flat,
            rows,
        ),
        check_vma=False,
    )
```

time: 852 us -> 534 us (0.63)
  waiting for transfers between devices: 399 us -> 135 us
  matrix products: 217 us -> 91.2 us
  Pallas kernels: 0 us -> 90.9 us
  blocking collectives: 82.3 us -> 0 us
  starting transfers between devices: 0.53 us -> 76.3 us
  between operations: 15.8 us -> 3.66 us
  other arithmetic: 66 us -> 54.9 us
  local copies, waits for them, and re-layouts: 63.4 us -> 73.2 us
    reduce_scatter x4 -> x0, waiting for transfers between devices: 295 us -> none  [the longest x1 142 us: reduce_forward(): lax.psum_scatter(up_grad, ('dp', 'inner'), scatter_dimension=0, tiled=True)]
    ppermute x0 -> x71, waiting for transfers between devices: none -> 135 us  [swap(): return lax.ppermute(value, AXES, [(i, i ^ mask) for i in range(self.count)])]
    dot_general x13 -> x0, matrix products: 113 us -> none  [the longest x2 29.9 us: attend_back(): jnp.einsum('qhd,khd->hqk', grad_mixed, value_rows, preferred_element_type...]
    all_gather x4 -> x0, waiting for transfers between devices: 102 us -> none  [the longest x1 53.6 us: fetch_forward(): lax.all_gather(w_down, ('dp', 'inner'), axis=0, tiled=True)]
    pallas_call x0 -> x6, Pallas kernels: none -> 90.9 us  [the longest x3 49.1 us: attention_backward(): pl.pallas_call(functools.partial(attention_backward_kernel, step), grid_s...]
    unnamed x2 -> x0, blocking collectives: 82.3 us -> none
    ppermute x0 -> x71, starting transfers between devices: none -> 76.3 us  [swap(): return lax.ppermute(value, AXES, [(i, i ^ mask) for i in range(self.count)])]
    concatenate x3 -> x42, other arithmetic: 1.55 us -> 26.9 us  [the longest x13 7.21 us: gather_inner(): rows = [jnp.concatenate([x, self.swap_inner(x, bit)], axis=0) for x in rows]]
  transfers between devices with their start and end apart: 8 -> 71, of which waited for: 6 -> 28; matrix products, arithmetic and copies ran while one was open for 34% -> 17% of each run, Pallas kernels for 0% -> 8%
where the time goes in v1:
time: 534 us; the launch traced here: 525 us
  waiting for transfers between devices  135 us (25%)
  matrix products  91.2 us (17%)
  Pallas kernels  90.9 us (17%)
  starting transfers between devices  76.3 us (14%)
  local copies, waits for them, and re-layouts  73.2 us (14%)
  other arithmetic  54.9 us (10%)
    ppermute x71, waiting for transfers between devices, swap(): return lax.ppermute(value, AXES, [(i, i ^ mask) for i in range(self.count)])  135 us
    ppermute x71, starting transfers between devices, swap(): return lax.ppermute(value, AXES, [(i, i ^ mask) for i in range(self.count)])  76.3 us
    pallas_call x3, Pallas kernels, attention_backward(): pl.pallas_call(functools.partial(attention_backward_kernel, step), grid_s...  49.1 us
    pallas_call x3, Pallas kernels, attention_forward(): pl.pallas_call(functools.partial(attention_forward_kernel, step), grid_sp...  41.9 us
    dot_general x4, matrix products, matmul_tr(): lax.dot_general(left, right, (((1,), (1,)), ((), ())), preferred_element_...  32.7 us
    dot_general x4, matrix products, tr_matmul(): lax.dot_general(left, right, (((0,), (0,)), ((), ())), preferred_element_...  30.7 us
    unnamed x236, local copies, waits for them, and re-layouts  30.2 us
    dot_general x4, matrix products, matmul(): return jnp.dot(left, right, preferred_element_type=jnp.float32)  27.8 us
  transfers between devices with their start and end apart: 71, of which 28 were waited for; matrix products, arithmetic and copies ran while one was open for 17% of the time, Pallas kernels for 8%

profile of v1, /device:TPU:0, one launch (start us, length us, event | category | flops | bytes accessed | tf_op | source)
XLA Modules:
  0.0 524.9 jit_solution(15335216746139100374)
XLA Ops:
  0.6 5.4 %concatenate.262 = bf16[288]{0:T(512)(128)(2,1)S(1)} concatenate(bf16[24]{0:T(256)(128)(2,1)} %param.18, bf16[24]{0:T(256)(128)(2,1)} %param.19, bf16[48]{0:T(256)(128)(2,1)} %param.21, bf16[24]{0:T(256)(128)(2,1)} %param.23, bf16[24]{0:T(256)(128)(2,1)} %param.24, bf16[24]{0:T(256)(128)(2,1)} %param.25, bf16[96]{0:T(256)(128)(2,1)} %param.27, bf16[24]{0:T(256)(128)(2,1)} %param.29), dimensions={0} | concatenate | bytes 1152 | tf_op jit(solution)/shard_map/concatenate | solution.py:363
  6.7 4.1 collective-permute-start
  12.1 2.9 collective-permute-start.20
  15.9 2.9 collective-permute-start.10
  32.5 2.4 collective-permute-done.2
  42.5 2.7 collective-permute-start.30
  55.4 2.8 collective-permute-done.21
  73.6 3.7 collective-permute-done.7
  84.1 8.4 %collective-permute-done.13 = bf16[2,96,1152]{2,1,0:T(8,128)(2,1)S(1)} collective-permute-done((bf16[2,96,1152]{2,1,0:T(8,128)(2,1)S(1)}, bf16[2,96,1152]{2,1,0:T(8,128)(2,1)S(1)}, u32[]{:S(2)}, u32[]{:S(2)}) %collective-permute-start.13) | collective-permute-done | bytes 442400 | tf_op jit(solution)/shard_map/ppermute | solution.py:71
  93.5 10.0 %collective-permute-done.32 = bf16[1,384,768]{2,1,0:T(8,128)(2,1)S(1)} collective-permute-done((bf16[1,384,768]{2,1,0:T(8,128)(2,1)S(1)}, bf16[1,384,768]{2,1,0:T(8,128)(2,1)S(1)}, u32[]{:S(2)}, u32[]{:S(2)}) %collective-permute-start.32) | collective-permute-done | bytes 589856 | tf_op jit(solution)/shard_map/ppermute | solution.py:71
  108.5 23.6 %collective-permute-done.28 = bf16[2,96,3072]{2,1,0:T(8,128)(2,1)S(1)} collective-permute-done((bf16[2,96,3072]{2,1,0:T(8,128)(2,1)S(1)}, bf16[2,96,3072]{2,1,0:T(8,128)(2,1)S(1)}, u32[]{:S(2)}, u32[]{:S(2)}) %collective-permute-start.28) | collective-permute-done | bytes 1179680 | tf_op jit(solution)/shard_map/ppermute | solution.py:71
  132.1 1.9 pad_maximum_fusion.3
  134.0 6.7 %add_convert_fusion.q_ref.k_ref.v_ref = bf16[1024,2304]{1,0:T(8,128)(2,1)} fusion(f32[2304]{0:T(1024)S(1)} %copy-done.75, bf16[768,1152]{1,0:T(8,128)(2,1)S(1)} %bitcast_dynamic-update-slice_fusion.16, bf16[768,1152]{1,0:T(8,128)(2,1)S(1)} %bitcast_dynamic-update-slice_fusion.24, bf16[1,1024,768]{1,2,0:T(8,128)(2,1)S(1)} %copy.38, f32[768]{0:T(1024)S(1)} %reshape.315, ...), kind=kOutput, calls=%fused_computation.12 | convolution fusion | flops 3640393728 | bytes 9853952 | tf_op jit(solution)/shard_map/dot_general | solution.py:43
  140.7 14.0 %attention_forward.3 = (bf16[1024,256]{1,0:T(8,128)(2,1)}, f32[2,2,1024]{2,1,0:T(2,128)}) custom-call(s32[1]{0:T(128)} %copy.102.count_ref, bf16[1024,2304]{1,0:T(8,128)(2,1)} %add_convert_fusion.q_ref.k_ref.v_ref, bf16[1024,2304]{1,0:T(8,128)(2,1)} %add_convert_fusion.q_ref.k_ref.v_ref, bf16[1024,2304]{1,0:T(8,128)(2,1)} %add_convert_fusion.q_ref.k_ref.v_ref), custom_call_target="tpu_custom_call" | custom-call | flops 2147483648 | bytes 2097152 | tf_op jit(solution)/shard_map/attention_forward/pallas_call | solution.py:219
  154.6 1.9 constant_dynamic-update-slice_fusion.5
  156.5 13.8 %attention_forward.4 = (bf16[1024,256]{1,0:T(8,128)(2,1)}, f32[2,2,1024]{2,1,0:T(2,128)}) custom-call(s32[1]{0:T(128)} %copy.102.count_ref, bf16[1024,2304]{1,0:T(8,128)(2,1)} %add_convert_fusion.q_ref.k_ref.v_ref, bf16[1024,2304]{1,0:T(8,128)(2,1)} %add_convert_fusion.q_ref.k_ref.v_ref, bf16[1024,2304]{1,0:T(8,128)(2,1)} %add_convert_fusion.q_ref.k_ref.v_ref), custom_call_target="tpu_custom_call" | custom-call | flops 2147483648 | bytes 2097152 | tf_op jit(solution)/shard_map/attention_forward/pallas_call | solution.py:219
  170.3 1.9 constant_dynamic-update-slice_fusion.4
  172.1 14.2 %attention_forward.5 = (bf16[1024,256]{1,0:T(8,128)(2,1)}, f32[2,2,1024]{2,1,0:T(2,128)}) custom-call(s32[1]{0:T(128)} %copy.102.count_ref, bf16[1024,2304]{1,0:T(8,128)(2,1)} %add_convert_fusion.q_ref.k_ref.v_ref, bf16[1024,2304]{1,0:T(8,128)(2,1)} %add_convert_fusion.q_ref.k_ref.v_ref, bf16[1024,2304]{1,0:T(8,128)(2,1)} %add_convert_fusion.q_ref.k_ref.v_ref), custom_call_target="tpu_custom_call" | custom-call | flops 2147483648 | bytes 2097152 | tf_op jit(solution)/shard_map/attention_forward/pallas_call | solution.py:219
  186.3 1.9 constant_dynamic-update-slice_fusion.3
  188.2 3.8 fusion.94
  194.9 1.9 pad_maximum_fusion
  197.2 2.1 collective-permute-done.34
  207.9 5.5 %fusion.90 = f32[1024,3072]{1,0:T(8,128)S(1)} fusion(bf16[768,3072]{1,0:T(8,128)(2,1)S(1)} %bitcast_dynamic-update-slice_fusion.8, f32[1024,768]{0,1:T(8,128)S(1)} %get-tuple-element.217, f32[768]{0:T(1024)S(1)} %copy-done.58, f32[768]{0:T(1024)S(1)} %copy-done.57, f32[1024]{0:T(1024)S(1)} %add_rsqrt_fusion, f32[1024]{0:T(1024)S(1)} %broadcast_multiply_fusion.4), kind=kOutput, calls=%fused_computation.393 | convolution fusion | flops 4835770368 | bytes 20461568 | tf_op jit(solution)/shard_map/dot_general | solution.py:43
  213.5 9.7 %convolution_convert_fusion = bf16[3072,768]{1,0:T(8,128)(2,1)} fusion(bf16[1,1024,768]{2,1,0:T(8,128)(2,1)S(1)} %copy-done.10, f32[1024,3072]{1,0:T(8,128)S(1)} %fusion.90, f32[3072]{0:T(1024)S(1)} %copy-done.74), kind=kOutput, calls=%fused_computation.13 | convolution fusion | flops 4865654784 | bytes 18886656 | tf_op jit(solution)/shard_map/dot_general | solution.py:53
  223.2 15.1 %fusion.97 = (bf16[3072]{0:T(1024)(128)(2,1)S(1)}, bf16[1024,3072]{1,0:T(8,128)(2,1)}) fusion(f32[1024,3072]{1,0:T(8,128)S(1)} %fusion.90, f32[3072]{0:T(1024)S(1)} %copy-done.74, bf16[3072,768]{1,0:T(8,128)(2,1)} %bitcast_dynamic-update-slice_fusion, bf16[1,1024,768]{2,1,0:T(8,128)(2,1)S(1)} %copy-done.10), kind=kOutput, calls=%fused_computation.400 | convolution fusion | flops 4897895424 | bytes 25184256 | tf_op jit(solution)/shard_map/dot_general | solution.py:47
  238.3 8.9 %fusion.96 = (bf16[768]{0:T(1024)(128)(2,1)S(1)}, f32[1024,768]{1,0:T(8,128)}) fusion(bf16[1024,3072]{1,0:T(8,128)(2,1)} %get-tuple-element.223, bf16[768,3072]{1,0:T(8,128)(2,1)S(1)} %bitcast_dynamic-update-slice_fusion.8), kind=kOutput, calls=%fused_computation.399 | convolution fusion | flops 4832623616 | bytes 14157312 | tf_op jit(solution)/shard_map/dot_general | solution.py:47
  247.2 7.1 %convolution_convert_fusion.1 = bf16[768,3072]{1,0:T(8,128)(2,1)} fusion(bf16[1024,3072]{1,0:T(8,128)(2,1)S(1)} %copy-done.86, f32[1024,768]{0,1:T(8,128)S(1)} %get-tuple-element.217, f32[768]{0:T(1024)S(1)} %copy-done.58, f32[768]{0:T(1024)S(1)} %copy-done.57, f32[1024]{0:T(1024)S(1)} %add_rsqrt_fusion, f32[1024]{0:T(1024)S(1)} %broadcast_multiply_fusion.4), kind=kOutput, calls=%fused_computation.14 | convolution fusion | flops 4838129664 | bytes 14170112 | tf_op jit(solution)/shard_map/dot_general | solution.py:53
  254.3 3.5 copy.41
  257.8 3.0 multiply_reduce_fusion
  261.1 2.0 convert_reduce_fusion.1
  263.1 5.1 convolution_convert_fusion.3
  268.2 2.7 multiply_convert_fusion.1.grad_ref
  270.9 16.5 %attention_backward.5 = (bf16[1024,256]{1,0:T(8,128)(2,1)}, bf16[1024,256]{1,0:T(8,128)(2,1)}, bf16[1024,256]{1,0:T(8,128)(2,1)}) custom-call(s32[1]{0:T(128)} %copy.102.count_ref, bf16[1024,2304]{1,0:T(8,128)(2,1)} %add_convert_fusion.q_ref.k_ref.v_ref, bf16[1024,2304]{1,0:T(8,128)(2,1)} %add_convert_fusion.q_ref.k_ref.v_ref, ...), custom_call_target="tpu_custom_call" | custom-call | flops 5368709120 | bytes 4194304 | tf_op jit(solution)/shard_map/attention_backward/pallas_call | solution.py:308
  287.5 16.2 %attention_backward.4 = (bf16[1024,256]{1,0:T(8,128)(2,1)}, bf16[1024,256]{1,0:T(8,128)(2,1)}, bf16[1024,256]{1,0:T(8,128)(2,1)}) custom-call(s32[1]{0:T(128)} %copy.102.count_ref, bf16[1024,2304]{1,0:T(8,128)(2,1)} %add_convert_fusion.q_ref.k_ref.v_ref, bf16[1024,2304]{1,0:T(8,128)(2,1)} %add_convert_fusion.q_ref.k_ref.v_ref, ...), custom_call_target="tpu_custom_call" | custom-call | flops 5368709120 | bytes 4194304 | tf_op jit(solution)/shard_map/attention_backward/pallas_call | solution.py:308
  303.6 16.3 %attention_backward.3 = (bf16[1024,256]{1,0:T(8,128)(2,1)}, bf16[1024,256]{1,0:T(8,128)(2,1)}, bf16[1024,256]{1,0:T(8,128)(2,1)}) custom-call(s32[1]{0:T(128)} %copy.102.count_ref, bf16[1024,2304]{1,0:T(8,128)(2,1)} %add_convert_fusion.q_ref.k_ref.v_ref, bf16[1024,2304]{1,0:T(8,128)(2,1)} %add_convert_fusion.q_ref.k_ref.v_ref, ...), custom_call_target="tpu_custom_call" | custom-call | flops 5368709120 | bytes 4194304 | tf_op jit(solution)/shard_map/attention_backward/pallas_call | solution.py:308
  323.9 2.4 copy-done.12
  327.3 6.1 %fusion.95 = (bf16[768]{0:T(1024)(128)(2,1)}, f32[1024,768]{1,0:T(8,128)}) fusion(bf16[1024,2304]{1,0:T(8,128)(2,1)S(1)} %constant_dynamic-update-slice_fusion.22, bf16[768,1152]{1,0:T(8,128)(2,1)S(1)} %copy-done.71, bf16[768,1152]{1,0:T(8,128)(2,1)S(1)} %copy-done.73), kind=kOutput, calls=%fused_computation.398 | convolution fusion | flops 3631742208 | bytes 11404800 | tf_op jit(solution)/shard_map/dot_general | solution.py:47
  333.4 3.6 reduce.1
  337.0 8.7 %convolution_convert_fusion.2 = bf16[768,2304]{1,0:T(8,128)(2,1)} fusion(bf16[1024,2304]{1,0:T(8,128)(2,1)} %copy-done.12, bf16[1,1024,768]{1,2,0:T(8,128)(2,1)} %copy-done, f32[768]{0:T(1024)S(1)} %copy-done.83, f32[768]{0:T(1024)S(1)} %copy-done.62, f32[1024]{0:T(1024)S(1)} %copy-done.63, f32[1024]{0:T(1024)S(1)} %copy-done.60), kind=kOutput, calls=%fused_computation.15 | convolution fusion | flops 3630366720 | bytes 9844736 | tf_op jit(solution)/shard_map/dot_general | solution.py:53
  345.7 11.8 %fusion.30 = bf16[1,1024,768]{1,2,0:T(8,128)(2,1)} fusion(f32[768]{0:T(1024)S(1)} %copy-done.81, f32[1024,768]{0,1:T(8,128)S(1)} %get-tuple-element.217, bf16[3072,768]{1,0:T(8,128)(2,1)} %bitcast_dynamic-update-slice_fusion, f32[1024,3072]{1,0:T(8,128)} %copy-done.3, f32[3072]{0:T(1024)S(1)} %copy-done.74), kind=kOutput, calls=%fused_computation.64 | convolution fusion | flops 4865654784 | bytes 22035456 | tf_op jit(solution)/shard_map/dot_general | solution.py:43
  357.5 2.8 copy.45
  361.6 4.0 dynamic-slice_bitcast_fusion.7
  367.4 2.5 dynamic-slice_bitcast_fusion.15
  377.8 3.7 copy.42
  381.6 3.0 fusion.23
  385.5 4.0 fusion.27
  390.8 1.9 collective-permute-start.36
  409.4 6.6 %collective-permute-done.54 = bf16[2,96,768]{2,1,0:T(8,128)(2,1)S(1)} collective-permute-done((bf16[2,96,768]{2,1,0:T(8,128)(2,1)S(1)}, bf16[2,96,768]{2,1,0:T(8,128)(2,1)S(1)}, u32[]{:S(2)}, u32[]{:S(2)}) %collective-permute-start.54) | collective-permute-done | bytes 294944 | tf_op jit(solution)/shard_map/ppermute | solution.py:71
  418.5 4.3 collective-permute-done.55
  426.9 3.4 collective-permute-done.58
  433.2 8.7 %collective-permute-done.42 = bf16[2,96,1152]{2,1,0:T(8,128)(2,1)S(1)} collective-permute-done((bf16[2,96,1152]{2,1,0:T(8,128)(2,1)S(1)}, bf16[2,96,1152]{2,1,0:T(8,128)(2,1)S(1)}, u32[]{:S(2)}, u32[]{:S(2)}) %collective-permute-start.42) | collective-permute-done | bytes 442400 | tf_op jit(solution)/shard_map/ppermute | solution.py:71
  441.9 1.9 collective-permute-start.43
  444.4 2.5 collective-permute-start.50
  449.0 2.5 collective-permute-start.44
  451.5 2.4 add_convert_fusion.4
  458.5 4.2 collective-permute-done.46
  463.6 16.7 %collective-permute-done.66 = bf16[2,384,768]{2,1,0:T(8,128)(2,1)S(1)} collective-permute-done((bf16[2,384,768]{2,1,0:T(8,128)(2,1)S(1)}, bf16[2,384,768]{2,1,0:T(8,128)(2,1)S(1)}, u32[]{:S(2)}, u32[]{:S(2)}) %collective-permute-start.66) | collective-permute-done | bytes 1179680 | tf_op jit(solution)/shard_map/ppermute | solution.py:71
  482.0 5.1 collective-permute-done.60
  487.9 8.6 %collective-permute-done.67 = bf16[1,384,768]{2,1,0:T(8,128)(2,1)S(1)} collective-permute-done((bf16[1,384,768]{2,1,0:T(8,128)(2,1)S(1)}, bf16[1,384,768]{2,1,0:T(8,128)(2,1)S(1)}, u32[]{:S(2)}, u32[]{:S(2)}) %collective-permute-start.67) | collective-permute-done | bytes 589856 | tf_op jit(solution)/shard_map/ppermute | solution.py:71
  496.8 2.7 collective-permute-start.68
  501.3 2.9 collective-permute-start.62
  504.6 3.1 collective-permute-done.68
  508.0 11.9 %collective-permute-done.69 = bf16[96,768]{1,0:T(8,128)(2,1)S(1)} collective-permute-done((bf16[96,768]{1,0:T(8,128)(2,1)S(1)}, bf16[96,768]{1,0:T(8,128)(2,1)S(1)}, u32[]{:S(2)}, u32[]{:S(2)}) %collective-permute-start.69) | collective-permute-done | bytes 147488 | tf_op jit(solution)/shard_map/ppermute | solution.py:71
  520.8 2.9 collective-permute-done.63
  (491 shorter events, 132.2 us)
Async XLA Ops:
  6.7 18.0 %collective-permute-start = (bf16[1,1,384]{2,1,0:T(2,128)(2,1)}, bf16[1,1,384]{2,1,0:T(2,128)(2,1)}, u32[]{:S(2)}, u32[]{:S(2)}) collective-permute-start(bf16[1,1,384]{2,1,0:T(2,128)(2,1)} %broadcast_in_dim_broadcast_in_dim.3), channel_id=1, source_target_pairs={{0,2},{1,3},{2,0},{3,1},{4,6},{5,7},{6,4},{7,5},{8,10},{9,11},{10,... | collective-permute-start | bytes 2312 | tf_op jit(solution)/shard_map/ppermute | solution.py:71
  12.1 33.8 %collective-permute-start.15 = (bf16[1,24,384]{2,1,0:T(8,128)(2,1)}, bf16[1,24,384]{2,1,0:T(8,128)(2,1)}, u32[]{:S(2)}, u32[]{:S(2)}) collective-permute-start(bf16[1,24,384]{2,1,0:T(8,128)(2,1)} %get-tuple-element.173), channel_id=1, source_target_pairs={{0,2},{1,3},{2,0},{3,1},{4,6},{5,7},{6,4},{7,5},{8,10},{9,11},{10,... | collective-permute-start | bytes 55304 | tf_op jit(solution)/shard_map/ppermute | solution.py:71
  12.1 30.4 %collective-permute-start.20 = (bf16[1,24,384]{2,1,0:T(8,128)(2,1)}, bf16[1,24,384]{2,1,0:T(8,128)(2,1)}, u32[]{:S(2)}, u32[]{:S(2)}) collective-permute-start(bf16[1,24,384]{2,1,0:T(8,128)(2,1)} %get-tuple-element.174), channel_id=1, source_target_pairs={{0,2},{1,3},{2,0},{3,1},{4,6},{5,7},{6,4},{7,5},{8,10},{9,11},{10,... | collective-permute-start | bytes 55304 | tf_op jit(solution)/shard_map/ppermute | solution.py:71
  15.9 43.7 %collective-permute-start.5 = (bf16[1,24,1152]{2,1,0:T(8,128)(2,1)S(1)}, bf16[1,24,1152]{2,1,0:T(8,128)(2,1)}, u32[]{:S(2)}, u32[]{:S(2)}) collective-permute-start(bf16[1,24,1152]{2,1,0:T(8,128)(2,1)S(1)} %get-tuple-element.163), channel_id=1, source_target_pairs={{0,2},{1,3},{2,0},{3,1},{4,6},{5,7},{6,4},{7,5},{8,10},{9,11},{10,... | collective-permute-start | bytes 165896 | tf_op jit(solution)/shard_map/ppermute | solution.py:71
  15.9 46.0 %collective-permute-start.10 = (bf16[1,24,1152]{2,1,0:T(8,128)(2,1)S(1)}, bf16[1,24,1152]{2,1,0:T(8,128)(2,1)}, u32[]{:S(2)}, u32[]{:S(2)}) collective-permute-start(bf16[1,24,1152]{2,1,0:T(8,128)(2,1)S(1)} %get-tuple-element.164), channel_id=1, source_target_pairs={{0,2},{1,3},{2,0},{3,1},{4,6},{5,7},{6,4},{7,5},{8,10},{9,11},{10,... | collective-permute-start | bytes 165896 | tf_op jit(solution)/shard_map/ppermute | solution.py:71
  36.2 5.2 collective-permute-start.3
  41.4 24.2 %collective-permute-start.25 = (bf16[1,24,3072]{2,1,0:T(8,128)(2,1)S(1)}, bf16[1,24,3072]{2,1,0:T(8,128)(2,1)S(1)}, u32[]{:S(2)}, u32[]{:S(2)}) collective-permute-start(bf16[1,24,3072]{2,1,0:T(8,128)(2,1)S(1)} %bitcast.464), channel_id=1, source_target_pairs={{0,2},{1,3},{2,0},{3,1},{4,6},{5,7},{6,4},{7,5},{8,10},{9,11},{10,... | collective-permute-start | bytes 442376 | tf_op jit(solution)/shard_map/ppermute | solution.py:71
  42.5 24.7 %collective-permute-start.30 = (bf16[1,96,768]{2,1,0:T(8,128)(2,1)S(1)}, bf16[1,96,768]{2,1,0:T(8,128)(2,1)S(1)}, u32[]{:S(2)}, u32[]{:S(2)}) collective-permute-start(bf16[1,96,768]{2,1,0:T(8,128)(2,1)S(1)} %bitcast.467), channel_id=1, source_target_pairs={{0,2},{1,3},{2,0},{3,1},{4,6},{5,7},{6,4},{7,5},{8,10},{9,11},{10,... | collective-permute-start | bytes 442376 | tf_op jit(solution)/shard_map/ppermute | solution.py:71
  47.2 7.0 %collective-permute-start.16 = (bf16[2,24,384]{2,1,0:T(8,128)(2,1)S(1)}, bf16[2,24,384]{2,1,0:T(8,128)(2,1)S(1)}, u32[]{:S(2)}, u32[]{:S(2)}) collective-permute-start(bf16[2,24,384]{2,1,0:T(8,128)(2,1)S(1)} %pad_maximum_fusion.40), channel_id=1, source_target_pairs={{0,1},{1,0},{2,3},{3,2},{4,5},{5,4},{6,7},{7,6},{8,9},{9,8},{10,11... | collective-permute-start | bytes 110600 | tf_op jit(solution)/shard_map/ppermute | solution.py:71
  59.0 4.4 collective-permute-start.22
  59.5 5.4 %collective-permute-start.17 = (bf16[1,96,384]{2,1,0:T(8,128)(2,1)S(1)}, bf16[1,96,384]{2,1,0:T(8,128)(2,1)S(1)}, u32[]{:S(2)}, u32[]{:S(2)}) collective-permute-start(bf16[1,96,384]{2,1,0:T(8,128)(2,1)S(1)} %maximum_bitcast_fusion.4), channel_id=1, source_target_pairs={{0,8},{1,9},{2,10},{3,11},{4,12},{5,13},{6,14},{7,15},{8,0},{9,1},... | collective-permute-start | bytes 221192 | tf_op jit(solution)/shard_map/ppermute | solution.py:71
  61.9 5.8 %collective-permute-start.6 = (bf16[2,24,1152]{2,1,0:T(8,128)(2,1)S(1)}, bf16[2,24,1152]{2,1,0:T(8,128)(2,1)S(1)}, u32[]{:S(2)}, u32[]{:S(2)}) collective-permute-start(bf16[2,24,1152]{2,1,0:T(8,128)(2,1)S(1)} %pad_maximum_fusion.36), channel_id=1, source_target_pairs={{0,1},{1,0},{2,3},{3,2},{4,5},{5,4},{6,7},{7,6},{8,9},{9,8},{10,11... | collective-permute-start | bytes 331784 | tf_op jit(solution)/shard_map/ppermute | solution.py:71
  63.4 6.9 %collective-permute-start.11 = (bf16[2,24,1152]{2,1,0:T(8,128)(2,1)S(1)}, bf16[2,24,1152]{2,1,0:T(8,128)(2,1)S(1)}, u32[]{:S(2)}, u32[]{:S(2)}) collective-permute-start(bf16[2,24,1152]{2,1,0:T(8,128)(2,1)S(1)} %pad_maximum_fusion.37), channel_id=1, source_target_pairs={{0,1},{1,0},{2,3},{3,2},{4,5},{5,4},{6,7},{7,6},{8,9},{9,8},{10,11... | collective-permute-start | bytes 331784 | tf_op jit(solution)/shard_map/ppermute | solution.py:71
  65.0 7.8 %collective-permute-start.23 = (bf16[2,96,384]{2,1,0:T(8,128)(2,1)S(1)}, bf16[2,96,384]{2,1,0:T(8,128)(2,1)S(1)}, u32[]{:S(2)}, u32[]{:S(2)}) collective-permute-start(bf16[2,96,384]{2,1,0:T(8,128)(2,1)S(1)} %pad_maximum_fusion.35), channel_id=1, source_target_pairs={{0,8},{1,9},{2,10},{3,11},{4,12},{5,13},{6,14},{7,15},{8,0},{9,1},... | collective-permute-start | bytes 442376 | tf_op jit(solution)/shard_map/ppermute | solution.py:71
  65.6 7.8 %collective-permute-start.18 = (bf16[2,96,384]{2,1,0:T(8,128)(2,1)S(1)}, bf16[2,96,384]{2,1,0:T(8,128)(2,1)S(1)}, u32[]{:S(2)}, u32[]{:S(2)}) collective-permute-start(bf16[2,96,384]{2,1,0:T(8,128)(2,1)S(1)} %pad_maximum_fusion.34), channel_id=1, source_target_pairs={{0,16},{1,17},{2,18},{3,19},{4,20},{5,21},{6,22},{7,23},{8,24},{9,... | collective-permute-start | bytes 442376 | tf_op jit(solution)/shard_map/ppermute | solution.py:71
  67.2 12.1 %collective-permute-start.26 = (bf16[2,24,3072]{2,1,0:T(8,128)(2,1)S(1)}, bf16[2,24,3072]{2,1,0:T(8,128)(2,1)S(1)}, u32[]{:S(2)}, u32[]{:S(2)}) collective-permute-start(bf16[2,24,3072]{2,1,0:T(8,128)(2,1)S(1)} %pad_maximum_fusion.29), channel_id=1, source_target_pairs={{0,1},{1,0},{2,3},{3,2},{4,5},{5,4},{6,7},{7,6},{8,9},{9,8},{10,11... | collective-permute-start | bytes 884744 | tf_op jit(solution)/shard_map/ppermute | solution.py:71
  67.8 13.0 %collective-permute-start.31 = (bf16[2,96,768]{2,1,0:T(8,128)(2,1)S(1)}, bf16[2,96,768]{2,1,0:T(8,128)(2,1)S(1)}, u32[]{:S(2)}, u32[]{:S(2)}) collective-permute-start(bf16[2,96,768]{2,1,0:T(8,128)(2,1)S(1)} %pad_maximum_fusion.30), channel_id=1, source_target_pairs={{0,1},{1,0},{2,3},{3,2},{4,5},{5,4},{6,7},{7,6},{8,9},{9,8},{10,11... | collective-permute-start | bytes 884744 | tf_op jit(solution)/shard_map/ppermute | solution.py:71
  71.2 6.0 %collective-permute-start.7 = (bf16[1,96,1152]{2,1,0:T(8,128)(2,1)S(1)}, bf16[1,96,1152]{2,1,0:T(8,128)(2,1)S(1)}, u32[]{:S(2)}, u32[]{:S(2)}) collective-permute-start(bf16[1,96,1152]{2,1,0:T(8,128)(2,1)S(1)} %maximum_bitcast_fusion.2), channel_id=1, source_target_pairs={{0,8},{1,9},{2,10},{3,11},{4,12},{5,13},{6,14},{7,15},{8,0},{9,1},... | collective-permute-start | bytes 663560 | tf_op jit(solution)/shard_map/ppermute | solution.py:71
  72.8 6.0 %collective-permute-start.12 = (bf16[1,96,1152]{2,1,0:T(8,128)(2,1)S(1)}, bf16[1,96,1152]{2,1,0:T(8,128)(2,1)S(1)}, u32[]{:S(2)}, u32[]{:S(2)}) collective-permute-start(bf16[1,96,1152]{2,1,0:T(8,128)(2,1)S(1)} %maximum_bitcast_fusion.3), channel_id=1, source_target_pairs={{0,16},{1,17},{2,18},{3,19},{4,20},{5,21},{6,22},{7,23},{8,24},{9,... | collective-permute-start | bytes 663560 | tf_op jit(solution)/shard_map/ppermute | solution.py:71
  73.4 10.4 %collective-permute-start.24 = (bf16[4,96,384]{2,1,0:T(8,128)(2,1)S(1)}, bf16[4,96,384]{2,1,0:T(8,128)(2,1)S(1)}, u32[]{:S(2)}, u32[]{:S(2)}) collective-permute-start(bf16[4,96,384]{2,1,0:T(8,128)(2,1)S(1)} %pad_maximum_fusion.28), channel_id=1, source_target_pairs={{0,4},{1,5},{2,6},{3,7},{4,0},{5,1},{6,2},{7,3},{8,12},{9,13},{10,... | collective-permute-start | bytes 884744 | tf_op jit(solution)/shard_map/ppermute | solution.py:71
  77.2 5.3 %collective-permute-start.19 = (bf16[4,96,384]{2,1,0:T(8,128)(2,1)S(1)}, bf16[4,96,384]{2,1,0:T(8,128)(2,1)S(1)}, u32[]{:S(2)}, u32[]{:S(2)}) collective-permute-start(bf16[4,96,384]{2,1,0:T(8,128)(2,1)S(1)} %pad_maximum_fusion.27), channel_id=1, source_target_pairs={{0,4},{1,5},{2,6},{3,7},{4,0},{5,1},{6,2},{7,3},{8,12},{9,13},{10,... | collective-permute-start | bytes 884744 | tf_op jit(solution)/shard_map/ppermute | solution.py:71
  78.8 13.9 %collective-permute-start.8 = (bf16[2,96,1152]{2,1,0:T(8,128)(2,1)S(1)}, bf16[2,96,1152]{2,1,0:T(8,128)(2,1)S(1)}, u32[]{:S(2)}, u32[]{:S(2)}) collective-permute-start(bf16[2,96,1152]{2,1,0:T(8,128)(2,1)S(1)} %pad_maximum_fusion.25), channel_id=1, source_target_pairs={{0,16},{1,17},{2,18},{3,19},{4,20},{5,21},{6,22},{7,23},{8,24},{9,... | collective-permute-start | bytes 1327112 | tf_op jit(solution)/shard_map/ppermute | solution.py:71
  79.4 13.1 %collective-permute-start.13 = (bf16[2,96,1152]{2,1,0:T(8,128)(2,1)S(1)}, bf16[2,96,1152]{2,1,0:T(8,128)(2,1)S(1)}, u32[]{:S(2)}, u32[]{:S(2)}) collective-permute-start(bf16[2,96,1152]{2,1,0:T(8,128)(2,1)S(1)} %pad_maximum_fusion.26), channel_id=1, source_target_pairs={{0,8},{1,9},{2,10},{3,11},{4,12},{5,13},{6,14},{7,15},{8,0},{9,1},... | collective-permute-start | bytes 1327112 | tf_op jit(solution)/shard_map/ppermute | solution.py:71
  81.0 22.6 %collective-permute-start.32 = (bf16[1,384,768]{2,1,0:T(8,128)(2,1)S(1)}, bf16[1,384,768]{2,1,0:T(8,128)(2,1)S(1)}, u32[]{:S(2)}, u32[]{:S(2)}) collective-permute-start(bf16[1,384,768]{2,1,0:T(8,128)(2,1)S(1)} %maximum_bitcast_fusion.1), channel_id=1, source_target_pairs={{0,8},{1,9},{2,10},{3,11},{4,12},{5,13},{6,14},{7,15},{8,0},{9,1},... | collective-permute-start | bytes 1769480 | tf_op jit(solution)/shard_map/ppermute | solution.py:71
  82.6 23.1 %collective-permute-start.27 = (bf16[1,96,3072]{2,1,0:T(8,128)(2,1)S(1)}, bf16[1,96,3072]{2,1,0:T(8,128)(2,1)S(1)}, u32[]{:S(2)}, u32[]{:S(2)}) collective-permute-start(bf16[1,96,3072]{2,1,0:T(8,128)(2,1)S(1)} %maximum_bitcast_fusion), channel_id=1, source_target_pairs={{0,16},{1,17},{2,18},{3,19},{4,20},{5,21},{6,22},{7,23},{8,24},{9,... | collective-permute-start | bytes 1769480 | tf_op jit(solution)/shard_map/ppermute | solution.py:71
  92.6 14.7 %collective-permute-start.14 = (bf16[4,96,1152]{2,1,0:T(8,128)(2,1)S(1)}, bf16[4,96,1152]{2,1,0:T(8,128)(2,1)S(1)}, u32[]{:S(2)}, u32[]{:S(2)}) collective-permute-start(bf16[4,96,1152]{2,1,0:T(8,128)(2,1)S(1)} %pad_maximum_fusion.15), channel_id=1, source_target_pairs={{0,4},{1,5},{2,6},{3,7},{4,0},{5,1},{6,2},{7,3},{8,12},{9,13},{10,... | collective-permute-start | bytes 2654216 | tf_op jit(solution)/shard_map/ppermute | solution.py:71
  92.8 15.0 %collective-permute-start.9 = (bf16[4,96,1152]{2,1,0:T(8,128)(2,1)S(1)}, bf16[4,96,1152]{2,1,0:T(8,128)(2,1)S(1)}, u32[]{:S(2)}, u32[]{:S(2)}) collective-permute-start(bf16[4,96,1152]{2,1,0:T(8,128)(2,1)S(1)} %pad_maximum_fusion.14), channel_id=1, source_target_pairs={{0,4},{1,5},{2,6},{3,7},{4,0},{5,1},{6,2},{7,3},{8,12},{9,13},{10,... | collective-permute-start | bytes 2654216 | tf_op jit(solution)/shard_map/ppermute | solution.py:71
  104.8 87.7 %collective-permute-start.33 = (bf16[2,384,768]{2,1,0:T(8,128)(2,1)}, bf16[2,384,768]{2,1,0:T(8,128)(2,1)}, u32[]{:S(2)}, u32[]{:S(2)}) collective-permute-start(bf16[2,384,768]{2,1,0:T(8,128)(2,1)} %pad_maximum_fusion.13), channel_id=1, source_target_pairs={{0,16},{1,17},{2,18},{3,19},{4,20},{5,21},{6,22},{7,23},{8,24},{9,... | collective-permute-start | bytes 3538952 | tf_op jit(solution)/shard_map/ppermute | solution.py:71
  105.8 26.3 %collective-permute-start.28 = (bf16[2,96,3072]{2,1,0:T(8,128)(2,1)S(1)}, bf16[2,96,3072]{2,1,0:T(8,128)(2,1)S(1)}, u32[]{:S(2)}, u32[]{:S(2)}) collective-permute-start(bf16[2,96,3072]{2,1,0:T(8,128)(2,1)S(1)} %pad_maximum_fusion.12), channel_id=1, source_target_pairs={{0,8},{1,9},{2,10},{3,11},{4,12},{5,13},{6,14},{7,15},{8,0},{9,1},... | collective-permute-start | bytes 3538952 | tf_op jit(solution)/shard_map/ppermute | solution.py:71
  133.9 60.9 %collective-permute-start.29 = (bf16[4,96,3072]{2,1,0:T(8,128)(2,1)}, bf16[4,96,3072]{2,1,0:T(8,128)(2,1)}, u32[]{:S(2)}, u32[]{:S(2)}) collective-permute-start(bf16[4,96,3072]{2,1,0:T(8,128)(2,1)} %pad_maximum_fusion.3), channel_id=1, source_target_pairs={{0,4},{1,5},{2,6},{3,7},{4,0},{5,1},{6,2},{7,3},{8,12},{9,13},{10,... | collective-permute-start | bytes 7077896 | tf_op jit(solution)/shard_map/ppermute | solution.py:71
  194.8 4.6 collective-permute-start.34
  367.4 81.6 %collective-permute-start.65 = (bf16[4,384,768]{2,1,0:T(8,128)(2,1)}, bf16[4,384,768]{2,1,0:T(8,128)(2,1)}, u32[]{:S(2)}, u32[]{:S(2)}) collective-permute-start(bf16[4,384,768]{2,1,0:T(8,128)(2,1)} %pad_maximum_fusion.6), channel_id=1, source_target_pairs={{0,4},{1,5},{2,6},{3,7},{4,0},{5,1},{6,2},{7,3},{8,12},{9,13},{10,... | collective-permute-start | bytes 7077896 | tf_op jit(solution)/shard_map/ppermute | solution.py:71
  385.0 5.8 %collective-permute-start.35 = (bf16[4,4,384]{2,1,0:T(4,128)(2,1)S(1)}, bf16[4,4,384]{2,1,0:T(4,128)(2,1)S(1)}, u32[]{:S(2)}, u32[]{:S(2)}) collective-permute-start(bf16[4,4,384]{2,1,0:T(4,128)(2,1)S(1)} %pad_maximum_fusion.45), channel_id=1, source_target_pairs={{0,4},{1,5},{2,6},{3,7},{4,0},{5,1},{6,2},{7,3},{8,12},{9,13},{10,... | collective-permute-start | bytes 36872 | tf_op jit(solution)/shard_map/ppermute | solution.py:71
  393.6 12.2 %collective-permute-start.53 = (bf16[4,96,768]{2,1,0:T(8,128)(2,1)}, bf16[4,96,768]{2,1,0:T(8,128)(2,1)}, u32[]{:S(2)}, u32[]{:S(2)}) collective-permute-start(bf16[4,96,768]{2,1,0:T(8,128)(2,1)} %pad_maximum_fusion.24), channel_id=1, source_target_pairs={{0,4},{1,5},{2,6},{3,7},{4,0},{5,1},{6,2},{7,3},{8,12},{9,13},{10,... | collective-permute-start | bytes 1769480 | tf_op jit(solution)/shard_map/ppermute | solution.py:71
  398.1 6.5 %collective-permute-start.38 = (bf16[1,384]{1,0:T(2,128)(2,1)S(1)}, bf16[1,384]{1,0:T(2,128)(2,1)S(1)}, u32[]{:S(2)}, u32[]{:S(2)}) collective-permute-start(bf16[1,384]{1,0:T(2,128)(2,1)S(1)} %get-tuple-element.207), channel_id=1, source_target_pairs={{0,1},{1,0},{2,3},{3,2},{4,5},{5,4},{6,7},{7,6},{8,9},{9,8},{10,11... | collective-permute-start | bytes 2312 | tf_op jit(solution)/shard_map/ppermute | solution.py:71
  398.9 5.8 %collective-permute-start.40 = (bf16[1,384]{1,0:T(2,128)(2,1)S(1)}, bf16[1,384]{1,0:T(2,128)(2,1)S(1)}, u32[]{:S(2)}, u32[]{:S(2)}) collective-permute-start(bf16[1,384]{1,0:T(2,128)(2,1)S(1)} %get-tuple-element.208), channel_id=1, source_target_pairs={{0,3},{1,2},{2,1},{3,0},{4,7},{5,6},{6,5},{7,4},{8,11},{9,10},{10,... | collective-permute-start | bytes 2312 | tf_op jit(solution)/shard_map/ppermute | solution.py:71
  400.2 5.0 collective-permute-start.39
  404.6 13.3 %collective-permute-start.47 = (bf16[4,96,1152]{2,1,0:T(8,128)(2,1)}, bf16[4,96,1152]{2,1,0:T(8,128)(2,1)S(1)}, u32[]{:S(2)}, u32[]{:S(2)}) collective-permute-start(bf16[4,96,1152]{2,1,0:T(8,128)(2,1)} %pad_maximum_fusion.17), channel_id=1, source_target_pairs={{0,4},{1,5},{2,6},{3,7},{4,0},{5,1},{6,2},{7,3},{8,12},{9,13},{10,... | collective-permute-start | bytes 2654216 | tf_op jit(solution)/shard_map/ppermute | solution.py:71
  404.7 21.3 %collective-permute-start.41 = (bf16[4,96,1152]{2,1,0:T(8,128)(2,1)}, bf16[4,96,1152]{2,1,0:T(8,128)(2,1)S(1)}, u32[]{:S(2)}, u32[]{:S(2)}) collective-permute-start(bf16[4,96,1152]{2,1,0:T(8,128)(2,1)} %pad_maximum_fusion.16), channel_id=1, source_target_pairs={{0,4},{1,5},{2,6},{3,7},{4,0},{5,1},{6,2},{7,3},{8,12},{9,13},{10,... | collective-permute-start | bytes 2654216 | tf_op jit(solution)/shard_map/ppermute | solution.py:71
  407.0 9.1 %collective-permute-start.54 = (bf16[2,96,768]{2,1,0:T(8,128)(2,1)S(1)}, bf16[2,96,768]{2,1,0:T(8,128)(2,1)S(1)}, u32[]{:S(2)}, u32[]{:S(2)}) collective-permute-start(bf16[2,96,768]{2,1,0:T(8,128)(2,1)S(1)} %get-tuple-element.137), channel_id=1, source_target_pairs={{0,16},{1,17},{2,18},{3,19},{4,20},{5,21},{6,22},{7,23},{8,24},{9,... | collective-permute-start | bytes 884744 | tf_op jit(solution)/shard_map/ppermute | solution.py:71
  416.1 6.7 %collective-permute-start.55 = (bf16[1,96,768]{2,1,0:T(8,128)(2,1)S(1)}, bf16[1,96,768]{2,1,0:T(8,128)(2,1)S(1)}, u32[]{:S(2)}, u32[]{:S(2)}) collective-permute-start(bf16[1,96,768]{2,1,0:T(8,128)(2,1)S(1)} %add_convert_fusion.26), channel_id=1, source_target_pairs={{0,8},{1,9},{2,10},{3,11},{4,12},{5,13},{6,14},{7,15},{8,0},{9,1},... | collective-permute-start | bytes 442376 | tf_op jit(solution)/shard_map/ppermute | solution.py:71
  418.2 14.5 %collective-permute-start.48 = (bf16[2,96,1152]{2,1,0:T(8,128)(2,1)S(1)}, bf16[2,96,1152]{2,1,0:T(8,128)(2,1)S(1)}, u32[]{:S(2)}, u32[]{:S(2)}) collective-permute-start(bf16[2,96,1152]{2,1,0:T(8,128)(2,1)S(1)} %get-tuple-element.129), channel_id=1, source_target_pairs={{0,8},{1,9},{2,10},{3,11},{4,12},{5,13},{6,14},{7,15},{8,0},{9,1},... | collective-permute-start | bytes 1327112 | tf_op jit(solution)/shard_map/ppermute | solution.py:71
  424.6 5.8 %collective-permute-start.58 = (bf16[24,768]{1,0:T(8,128)(2,1)S(1)}, bf16[24,768]{1,0:T(8,128)(2,1)S(1)}, u32[]{:S(2)}, u32[]{:S(2)}) collective-permute-start(bf16[24,768]{1,0:T(8,128)(2,1)S(1)} %get-tuple-element.161), channel_id=1, source_target_pairs={{0,3},{1,2},{2,1},{3,0},{4,7},{5,6},{6,5},{7,4},{8,11},{9,10},{10,... | collective-permute-start | bytes 110600 | tf_op jit(solution)/shard_map/ppermute | solution.py:71
  426.0 6.1 %collective-permute-start.57 = (bf16[24,768]{1,0:T(8,128)(2,1)S(1)}, bf16[24,768]{1,0:T(8,128)(2,1)S(1)}, u32[]{:S(2)}, u32[]{:S(2)}) collective-permute-start(bf16[24,768]{1,0:T(8,128)(2,1)S(1)} %get-tuple-element.162), channel_id=1, source_target_pairs={{0,2},{1,3},{2,0},{3,1},{4,6},{5,7},{6,4},{7,5},{8,10},{9,11},{10,... | collective-permute-start | bytes 110600 | tf_op jit(solution)/shard_map/ppermute | solution.py:71
  426.9 27.0 %collective-permute-start.59 = (bf16[4,96,3072]{2,1,0:T(8,128)(2,1)S(1)}, bf16[4,96,3072]{2,1,0:T(8,128)(2,1)S(1)}, u32[]{:S(2)}, u32[]{:S(2)}) collective-permute-start(bf16[4,96,3072]{2,1,0:T(8,128)(2,1)S(1)} %copy-done.20), channel_id=1, source_target_pairs={{0,4},{1,5},{2,6},{3,7},{4,0},{5,1},{6,2},{7,3},{8,12},{9,13},{10,... | collective-permute-start | bytes 7077896 | tf_op jit(solution)/shard_map/ppermute | solution.py:71
  430.4 11.5 %collective-permute-start.42 = (bf16[2,96,1152]{2,1,0:T(8,128)(2,1)S(1)}, bf16[2,96,1152]{2,1,0:T(8,128)(2,1)S(1)}, u32[]{:S(2)}, u32[]{:S(2)}) collective-permute-start(bf16[2,96,1152]{2,1,0:T(8,128)(2,1)S(1)} %get-tuple-element.127), channel_id=1, source_target_pairs={{0,16},{1,17},{2,18},{3,19},{4,20},{5,21},{6,22},{7,23},{8,24},{9,... | collective-permute-start | bytes 1327112 | tf_op jit(solution)/shard_map/ppermute | solution.py:71
  432.8 11.5 %collective-permute-start.49 = (bf16[1,96,1152]{2,1,0:T(8,128)(2,1)S(1)}, bf16[1,96,1152]{2,1,0:T(8,128)(2,1)S(1)}, u32[]{:S(2)}, u32[]{:S(2)}) collective-permute-start(bf16[1,96,1152]{2,1,0:T(8,128)(2,1)S(1)} %add_convert_fusion.20), channel_id=1, source_target_pairs={{0,16},{1,17},{2,18},{3,19},{4,20},{5,21},{6,22},{7,23},{8,24},{9,... | collective-permute-start | bytes 663560 | tf_op jit(solution)/shard_map/ppermute | solution.py:71
  441.9 6.3 %collective-permute-start.43 = (bf16[1,96,1152]{2,1,0:T(8,128)(2,1)S(1)}, bf16[1,96,1152]{2,1,0:T(8,128)(2,1)S(1)}, u32[]{:S(2)}, u32[]{:S(2)}) collective-permute-start(bf16[1,96,1152]{2,1,0:T(8,128)(2,1)S(1)} %add_convert_fusion.23), channel_id=1, source_target_pairs={{0,8},{1,9},{2,10},{3,11},{4,12},{5,13},{6,14},{7,15},{8,0},{9,1},... | collective-permute-start | bytes 663560 | tf_op jit(solution)/shard_map/ppermute | solution.py:71
  444.4 12.2 %collective-permute-start.50 = (bf16[24,1152]{1,0:T(8,128)(2,1)S(1)}, bf16[24,1152]{1,0:T(8,128)(2,1)S(1)}, u32[]{:S(2)}, u32[]{:S(2)}) collective-permute-start(bf16[24,1152]{1,0:T(8,128)(2,1)S(1)} %get-tuple-element.149), channel_id=1, source_target_pairs={{0,1},{1,0},{2,3},{3,2},{4,5},{5,4},{6,7},{7,6},{8,9},{9,8},{10,11... | collective-permute-start | bytes 165896 | tf_op jit(solution)/shard_map/ppermute | solution.py:71
  446.9 10.5 %collective-permute-start.52 = (bf16[24,1152]{1,0:T(8,128)(2,1)S(1)}, bf16[24,1152]{1,0:T(8,128)(2,1)S(1)}, u32[]{:S(2)}, u32[]{:S(2)}) collective-permute-start(bf16[24,1152]{1,0:T(8,128)(2,1)S(1)} %get-tuple-element.150), channel_id=1, source_target_pairs={{0,3},{1,2},{2,1},{3,0},{4,7},{5,6},{6,5},{7,4},{8,11},{9,10},{10,... | collective-permute-start | bytes 165896 | tf_op jit(solution)/shard_map/ppermute | solution.py:71
  448.3 9.9 %collective-permute-start.51 = (bf16[24,1152]{1,0:T(8,128)(2,1)S(1)}, bf16[24,1152]{1,0:T(8,128)(2,1)S(1)}, u32[]{:S(2)}, u32[]{:S(2)}) collective-permute-start(bf16[24,1152]{1,0:T(8,128)(2,1)S(1)} %get-tuple-element.151), channel_id=1, source_target_pairs={{0,2},{1,3},{2,0},{3,1},{4,6},{5,7},{6,4},{7,5},{8,10},{9,11},{10,... | collective-permute-start | bytes 165896 | tf_op jit(solution)/shard_map/ppermute | solution.py:71
  449.0 9.5 %collective-permute-start.44 = (bf16[24,1152]{1,0:T(8,128)(2,1)S(1)}, bf16[24,1152]{1,0:T(8,128)(2,1)S(1)}, u32[]{:S(2)}, u32[]{:S(2)}) collective-permute-start(bf16[24,1152]{1,0:T(8,128)(2,1)S(1)} %get-tuple-element.146), channel_id=1, source_target_pairs={{0,1},{1,0},{2,3},{3,2},{4,5},{5,4},{6,7},{7,6},{8,9},{9,8},{10,11... | collective-permute-start | bytes 165896 | tf_op jit(solution)/shard_map/ppermute | solution.py:71
  453.9 26.4 %collective-permute-start.66 = (bf16[2,384,768]{2,1,0:T(8,128)(2,1)S(1)}, bf16[2,384,768]{2,1,0:T(8,128)(2,1)S(1)}, u32[]{:S(2)}, u32[]{:S(2)}) collective-permute-start(bf16[2,384,768]{2,1,0:T(8,128)(2,1)S(1)} %get-tuple-element.99), channel_id=1, source_target_pairs={{0,16},{1,17},{2,18},{3,19},{4,20},{5,21},{6,22},{7,23},{8,24},{9,... | collective-permute-start | bytes 3538952 | tf_op jit(solution)/shard_map/ppermute | solution.py:71
  456.6 6.1 %collective-permute-start.46 = (bf16[24,1152]{1,0:T(8,128)(2,1)S(1)}, bf16[24,1152]{1,0:T(8,128)(2,1)S(1)}, u32[]{:S(2)}, u32[]{:S(2)}) collective-permute-start(bf16[24,1152]{1,0:T(8,128)(2,1)S(1)} %get-tuple-element.147), channel_id=1, source_target_pairs={{0,3},{1,2},{2,1},{3,0},{4,7},{5,6},{6,5},{7,4},{8,11},{9,10},{10,... | collective-permute-start | bytes 165896 | tf_op jit(solution)/shard_map/ppermute | solution.py:71
  457.3 6.2 %collective-permute-start.45 = (bf16[24,1152]{1,0:T(8,128)(2,1)S(1)}, bf16[24,1152]{1,0:T(8,128)(2,1)S(1)}, u32[]{:S(2)}, u32[]{:S(2)}) collective-permute-start(bf16[24,1152]{1,0:T(8,128)(2,1)S(1)} %get-tuple-element.148), channel_id=1, source_target_pairs={{0,2},{1,3},{2,0},{3,1},{4,6},{5,7},{6,4},{7,5},{8,10},{9,11},{10,... | collective-permute-start | bytes 165896 | tf_op jit(solution)/shard_map/ppermute | solution.py:71
  458.2 28.8 %collective-permute-start.60 = (bf16[2,96,3072]{2,1,0:T(8,128)(2,1)S(1)}, bf16[2,96,3072]{2,1,0:T(8,128)(2,1)S(1)}, u32[]{:S(2)}, u32[]{:S(2)}) collective-permute-start(bf16[2,96,3072]{2,1,0:T(8,128)(2,1)S(1)} %get-tuple-element.101), channel_id=1, source_target_pairs={{0,8},{1,9},{2,10},{3,11},{4,12},{5,13},{6,14},{7,15},{8,0},{9,1},... | collective-permute-start | bytes 3538952 | tf_op jit(solution)/shard_map/ppermute | solution.py:71
  480.4 16.1 %collective-permute-start.67 = (bf16[1,384,768]{2,1,0:T(8,128)(2,1)S(1)}, bf16[1,384,768]{2,1,0:T(8,128)(2,1)S(1)}, u32[]{:S(2)}, u32[]{:S(2)}) collective-permute-start(bf16[1,384,768]{2,1,0:T(8,128)(2,1)S(1)} %add_convert_fusion.8), channel_id=1, source_target_pairs={{0,8},{1,9},{2,10},{3,11},{4,12},{5,13},{6,14},{7,15},{8,0},{9,1},... | collective-permute-start | bytes 1769480 | tf_op jit(solution)/shard_map/ppermute | solution.py:71
  487.2 13.9 %collective-permute-start.61 = (bf16[1,96,3072]{2,1,0:T(8,128)(2,1)S(1)}, bf16[1,96,3072]{2,1,0:T(8,128)(2,1)S(1)}, u32[]{:S(2)}, u32[]{:S(2)}) collective-permute-start(bf16[1,96,3072]{2,1,0:T(8,128)(2,1)S(1)} %add_convert_fusion.11), channel_id=1, source_target_pairs={{0,16},{1,17},{2,18},{3,19},{4,20},{5,21},{6,22},{7,23},{8,24},{9,... | collective-permute-start | bytes 1769480 | tf_op jit(solution)/shard_map/ppermute | solution.py:71
  496.8 10.8 %collective-permute-start.68 = (bf16[96,768]{1,0:T(8,128)(2,1)S(1)}, bf16[96,768]{1,0:T(8,128)(2,1)S(1)}, u32[]{:S(2)}, u32[]{:S(2)}) collective-permute-start(bf16[96,768]{1,0:T(8,128)(2,1)S(1)} %get-tuple-element.130), channel_id=1, source_target_pairs={{0,1},{1,0},{2,3},{3,2},{4,5},{5,4},{6,7},{7,6},{8,9},{9,8},{10,11... | collective-permute-start | bytes 442376 | tf_op jit(solution)/shard_map/ppermute | solution.py:71
  499.5 8.5 %collective-permute-start.70 = (bf16[96,768]{1,0:T(8,128)(2,1)S(1)}, bf16[96,768]{1,0:T(8,128)(2,1)S(1)}, u32[]{:S(2)}, u32[]{:S(2)}) collective-permute-start(bf16[96,768]{1,0:T(8,128)(2,1)S(1)} %get-tuple-element.131), channel_id=1, source_target_pairs={{0,3},{1,2},{2,1},{3,0},{4,7},{5,6},{6,5},{7,4},{8,11},{9,10},{10,... | collective-permute-start | bytes 442376 | tf_op jit(solution)/shard_map/ppermute | solution.py:71
  499.9 20.1 %collective-permute-start.69 = (bf16[96,768]{1,0:T(8,128)(2,1)S(1)}, bf16[96,768]{1,0:T(8,128)(2,1)S(1)}, u32[]{:S(2)}, u32[]{:S(2)}) collective-permute-start(bf16[96,768]{1,0:T(8,128)(2,1)S(1)} %get-tuple-element.132), channel_id=1, source_target_pairs={{0,2},{1,3},{2,0},{3,1},{4,6},{5,7},{6,4},{7,5},{8,10},{9,11},{10,... | collective-permute-start | bytes 442376 | tf_op jit(solution)/shard_map/ppermute | solution.py:71
  501.3 19.4 %collective-permute-start.62 = (bf16[24,3072]{1,0:T(8,128)(2,1)S(1)}, bf16[24,3072]{1,0:T(8,128)(2,1)S(1)}, u32[]{:S(2)}, u32[]{:S(2)}) collective-permute-start(bf16[24,3072]{1,0:T(8,128)(2,1)S(1)} %get-tuple-element.133), channel_id=1, source_target_pairs={{0,1},{1,0},{2,3},{3,2},{4,5},{5,4},{6,7},{7,6},{8,9},{9,8},{10,11... | collective-permute-start | bytes 442376 | tf_op jit(solution)/shard_map/ppermute | solution.py:71
  504.2 16.5 %collective-permute-start.64 = (bf16[24,3072]{1,0:T(8,128)(2,1)S(1)}, bf16[24,3072]{1,0:T(8,128)(2,1)S(1)}, u32[]{:S(2)}, u32[]{:S(2)}) collective-permute-start(bf16[24,3072]{1,0:T(8,128)(2,1)S(1)} %get-tuple-element.134), channel_id=1, source_target_pairs={{0,3},{1,2},{2,1},{3,0},{4,7},{5,6},{6,5},{7,4},{8,11},{9,10},{10,... | collective-permute-start | bytes 442376 | tf_op jit(solution)/shard_map/ppermute | solution.py:71
  507.7 16.0 %collective-permute-start.63 = (bf16[24,3072]{1,0:T(8,128)(2,1)S(1)}, bf16[24,3072]{1,0:T(8,128)(2,1)S(1)}, u32[]{:S(2)}, u32[]{:S(2)}) collective-permute-start(bf16[24,3072]{1,0:T(8,128)(2,1)S(1)} %get-tuple-element.135), channel_id=1, source_target_pairs={{0,2},{1,3},{2,0},{3,1},{4,6},{5,7},{6,4},{7,5},{8,10},{9,11},{10,... | collective-permute-start | bytes 442376 | tf_op jit(solution)/shard_map/ppermute | solution.py:71
  (96 other events, 1148.0 us)
